TPU v7x, 32 devices: a whole 2x2x4 slice. The times are simulated.
32 devices in a mesh: row: 4 (over x, core), col: 2 (over y), store: 4 (over z).
Axes of the slice: x: 2, y: 2, z: 4, core: 2. Of those that a mesh axis runs over, the one named last changes fastest.
Arguments:
- hidden: bfloat16 [128, 128, 4096], P('store', 'row', 'col'), may hold values from -6 to 6
- out_grads: bfloat16 [208, 128, 128], P('row', 'store'), may hold values from -6 to 6
- proj_out: bfloat16 [208, 64], P('row'), may hold values from -0.4375 to 0.4375
- proj_in: bfloat16 [4096, 64], P('col'), may hold values from -0.09375 to 0.09375
- lengths: int32 [128], P('store'), may hold values from 64 to 128
- precond: bfloat16 [4096, 4096], P(('row', 'col'), 'store'), may hold values from -1 to 2, as said below
- stored: bfloat16 [12288, 4096], P(('row', 'col', 'store')), may hold values from -0.09375 to 0.09375
Outputs:
- scores: float32 [128, 12288], P(None, ('row', 'col', 'store'))
Inputs may be any that keep to these rules, and one draw needn't show every extreme that they name: Query q's live tokens are its first lengths[q] token slots. precond is symmetric.
All inputs are finite; a program needn't handle non-finite values.
Results may differ from a plain program's by a relative error of at most 0.0057.
Values may be sent and summed in bfloat16 or wider, within the bound.
No kernel may reach another device: no remote copies, remote signals or barrier semaphores. Data moves between devices by JAX's collectives and lax.ppermute only.
A program may use at most 64 MiB of HBM per device.

v0:
```python
import jax
import jax.numpy as jnp
from jax import lax
from jax.sharding import PartitionSpec as P

TOK = 128


def on_device(hidden, out_grads, proj_out, proj_in, lengths, precond, stored):
    queries, token_part, columns = hidden.shape
    width_in = proj_in.shape[1]
    local_proj = jnp.einsum(
        "qtc,cb->qtb", hidden, proj_in, preferred_element_type=jnp.float32
    ).astype(jnp.bfloat16)
    flattened = local_proj.reshape(queries, token_part * width_in)
    inputs_all = lax.all_gather(flattened, "row", axis=1, tiled=True).reshape(queries, -1, width_in)
    tokens = inputs_all.shape[1]
    position = jnp.arange(tokens, dtype=jnp.int32)
    live_mask = (position[None, :] < lengths[:, None]).astype(jnp.float32)
    outputs_proj = jnp.einsum(
        "rqt,ra->qta", out_grads, proj_out, preferred_element_type=jnp.float32
    )
    outputs_proj = (outputs_proj * live_mask[:, :, None]).astype(jnp.bfloat16)
    partial_value = jnp.einsum(
        "qta,qtb->qab", outputs_proj, inputs_all, preferred_element_type=jnp.float32
    )
    partial_value = partial_value.reshape(queries, -1) * TOK ** (-0.5)
    shares = lax.psum_scatter(
        partial_value, ("row", "col"), scatter_dimension=1, tiled=True
    ).astype(jnp.bfloat16)
    cond_terms = jnp.dot(
        shares,
        lax.all_gather(precond, "store", axis=1, tiled=True),
        preferred_element_type=jnp.float32,
    )
    conditioned = lax.psum_scatter(
        cond_terms, ("row", "col"), scatter_dimension=1, tiled=True
    ).astype(jnp.bfloat16)
    full_features = lax.all_gather(conditioned, ("row", "col"), axis=1, tiled=True)
    return lax.dot_general(
        lax.all_gather(full_features, "store", axis=0, tiled=True),
        stored,
        (((1,), (1,)), ((), ())),
        preferred_element_type=jnp.float32,
    )


def solution(mesh):
    return jax.shard_map(
        on_device,
        mesh=mesh,
        in_specs=(
            P("store", "row", "col"),
            P("row", "store", None),
            P("row", None),
            P("col", None),
            P("store"),
            P(("row", "col"), "store"),
            P(("row", "col", "store"), None),
        ),
        out_specs=P(None, ("row", "col", "store")),
        check_vma=False,
    )
```

profile of v0, /device:TPU:0, one launch (start us, length us, event | category | flops | bytes accessed | tf_op | source)
XLA Modules:
  0.0 207.3 jit_solution(10469774446894021144)
XLA Ops:
  7.4 0.0 copy-start
  7.4 0.0 reduce-scatter.3.cloned.1.call-start
  7.4 3.6 %convolution_convert_fusion = bf16[32,32,64]{2,1,0:T(8,128)(2,1)S(1)} fusion(bf16[32,32,2048]{2,1,0:T(8,128)(2,1)} %param.7, bf16[2048,64]{0,1:T(8,128)(2,1)} %param.10), kind=kOutput, calls=%fused_computation.3 | convolution fusion | flops 268500992 | bytes 4587520 | tf_op jit(solution)/shard_map/qtc,cb->qtb/dot_general | solution.py:12
  11.0 0.3 reshape.31
  11.3 9.1 %all_gather.12 = bf16[32,8192]{1,0:T(8,128)(2,1)} all-gather(bf16[32,2048]{1,0:T(8,128)(2,1)S(1)} %reshape.31), channel_id=1, replica_groups=mesh['row'=4,'col'=2,'store'=4] {'row'}, dimensions={1}, use_global_device_ids=true | all-gather | bytes 655360 | tf_op jit(solution)/shard_map/all_gather | solution.py:16
  20.3 2.7 %reshape.32 = bf16[32,128,64]{2,1,0:T(8,128)(2,1)} reshape(bf16[32,8192]{1,0:T(8,128)(2,1)} %all_gather.12) | data formatting | bytes 1048576 | tf_op jit(solution)/shard_map/reshape | solution.py:16
  23.1 0.7 fusion.7
  23.8 3.0 %convolution_multiply_fusion.1 = f32[32,64,64]{2,1,0:T(8,128)} fusion(bf16[32,128,64]{2,1,0:T(8,128)(2,1)} %reshape.32, f32[32,128]{1,0:T(8,128)S(1)} %fusion.7, bf16[52,32,128]{2,1,0:T(8,128)(2,1)} %param.8, bf16[52,64]{1,0:T(8,128)(2,1)S(1)} %copy-done.1), kind=kOutput, calls=%fused_computation.1 | convolution fusion | flops 61472768 | bytes 1497600 | tf_op jit(solution)/shard_map/qta,qtb->qab/dot_general | solution.py:24
  26.8 2.4 %mul.21 = f32[32,4096]{1,0:T(8,128)} reshape(f32[32,64,64]{2,1,0:T(8,128)} %convolution_multiply_fusion.1) | data formatting | bytes 1048576 | tf_op jit(solution)/shard_map/mul | solution.py:27
  29.2 0.0 reduce-scatter.3.cloned.1.call-update
  29.3 0.0 all-gather.3.cloned.1.call-start
  29.3 0.5 all-gather.3.cloned.1.call-update
  29.8 0.0 reduce-scatter.5.cloned.1.call-start
  29.9 34.5 %reduce-scatter.3.cloned.1.call-done = f32[32,512]{1,0:T(8,128)} async-done(((f32[32,4096]{1,0:T(8,128)}), f32[32,512]{1,0:T(8,128)}) %reduce-scatter.3.cloned.1.call-update) | async-done | bytes 65552 | tf_op jit(solution)/shard_map/reduce_scatter | solution.py:28
  64.4 48.4 %all-gather.3.cloned.1.call-done = bf16[512,4096]{1,0:T(8,128)(2,1)} async-done(((bf16[512,1024]{1,0:T(8,128)(2,1)}), bf16[512,4096]{1,0:T(8,128)(2,1)}) %all-gather.3.cloned.1.call-update) | async-done | bytes 4194320 | tf_op jit(solution)/shard_map/all_gather | solution.py:33
  112.8 3.9 %fusion.5 = f32[32,4096]{1,0:T(8,128)} fusion(bf16[512,4096]{1,0:T(8,128)(2,1)} %all-gather.3.cloned.1.call-done, f32[32,512]{1,0:T(8,128)} %reduce-scatter.3.cloned.1.call-done), kind=kOutput, calls=%fused_computation.7 | convolution fusion | flops 134234112 | bytes 4784128 | tf_op jit(solution)/shard_map/dot_general | solution.py:31
  116.7 0.0 reduce-scatter.5.cloned.1.call-update
  116.7 0.0 all-gather.5.cloned.1.call-start
  116.7 32.7 %reduce-scatter.5.cloned.1.call-done = f32[32,512]{1,0:T(8,128)} async-done(((f32[32,4096]{1,0:T(8,128)}), f32[32,512]{1,0:T(8,128)}) %reduce-scatter.5.cloned.1.call-update) | async-done | bytes 65552 | tf_op jit(solution)/shard_map/reduce_scatter | solution.py:36
  149.4 0.8 convert_element_type.23
  150.3 18.6 %all_gather.14 = bf16[32,4096]{1,0:T(8,128)(2,1)} all-gather(bf16[32,512]{1,0:T(8,128)(2,1)S(1)} %convert_element_type.23), channel_id=1, replica_groups=mesh['row'=4,'col'=2,'store'=4] {'row','col'}, dimensions={1}, use_global_device_ids=true | all-gather | bytes 294912 | tf_op jit(solution)/shard_map/all_gather | solution.py:39
  168.9 0.0 all-gather.5.cloned.1.call-update
  168.9 28.0 %all-gather.5.cloned.1.call-done = bf16[128,4096]{1,0:T(8,128)(2,1)} async-done(((bf16[32,4096]{1,0:T(8,128)(2,1)}), bf16[128,4096]{1,0:T(8,128)(2,1)}) %all-gather.5.cloned.1.call-update) | async-done | bytes 1048592 | tf_op jit(solution)/shard_map/all_gather | solution.py:41
  196.9 3.0 %fusion.10 = f32[128,384]{1,0:T(8,128)} fusion(bf16[128,4096]{1,0:T(8,128)(2,1)} %all-gather.5.cloned.1.call-done, bf16[384,4096]{1,0:T(8,128)(2,1)S(1)} %copy-done), kind=kOutput, calls=%fused_computation.12 | convolution fusion | flops 402653184 | bytes 4390912 | tf_op jit(solution)/shard_map/dot_general | solution.py:40
  (3 shorter events, 0.0 us)
Async XLA Ops:
  7.4 189.6 %copy-start = (bf16[384,4096]{1,0:T(8,128)(2,1)S(1)}, bf16[384,4096]{1,0:T(8,128)(2,1)}, u32[]{:S(2)}) copy-start(bf16[384,4096]{1,0:T(8,128)(2,1)} %param.13) | copy-start | bytes 9437188
  7.4 16.5 %copy-start.1 = (bf16[52,64]{1,0:T(8,128)(2,1)S(1)}, bf16[52,64]{1,0:T(8,128)(2,1)}, u32[]{:S(2)}) copy-start(bf16[52,64]{1,0:T(8,128)(2,1)} %param.9) | copy-start | bytes 19972
  7.4 57.0 %reduce-scatter.3.cloned.1.call-start = ((), (), s32[]{:S(2)}) async-start(), calls=%async_computation.2 | async-start | bytes 589824 | tf_op jit(solution)/shard_map/reduce_scatter | solution.py:28
  29.3 83.5 %all-gather.3.cloned.1.call-start = ((), (), s32[]{:S(2)}) async-start(), calls=%async_computation.3 | async-start | bytes 5242880 | tf_op jit(solution)/shard_map/all_gather | solution.py:33
  29.8 119.6 %reduce-scatter.5.cloned.1.call-start = ((), (), s32[]{:S(2)}) async-start(), calls=%async_computation.4 | async-start | bytes 589824 | tf_op jit(solution)/shard_map/reduce_scatter | solution.py:36
  116.7 80.2 %all-gather.5.cloned.1.call-start = ((), (), s32[]{:S(2)}) async-start(), calls=%async_computation.5 | async-start | bytes 1310720 | tf_op jit(solution)/shard_map/all_gather | solution.py:41
Sparse Core Ops, SparseCore 0:
  29.4 34.9 reduce-scatter.2
  116.8 32.5 reduce-scatter.4
Sparse Core Ops, SparseCore 1:
  31.3 81.4 all-gather.2
  169.0 27.9 all-gather.4
where the time goes:
time: 208 us; the launch traced here: 207 us
  waiting for transfers between devices  144 us (69%)
  blocking collectives  27.7 us (13%)
  between operations  14.9 us (7%)
  matrix products  13.4 us (6%)
  local copies, waits for them, and re-layouts  5.42 us (3%)
    all_gather x1, waiting for transfers between devices, on_device(): lax.all_gather(precond, 'store', axis=1, tiled=True)  48.4 us
    reduce_scatter x1, waiting for transfers between devices, on_device(): lax.psum_scatter(partial_value, ('row', 'col'), scatter_dimension=1, tile...  34.5 us
    reduce_scatter x1, waiting for transfers between devices, on_device(): lax.psum_scatter(cond_terms, ('row', 'col'), scatter_dimension=1, tiled=T...  32.7 us
    all_gather x1, waiting for transfers between devices, on_device(): lax.all_gather(full_features, 'store', axis=0, tiled=True)  28 us
    all_gather x1, blocking collectives, on_device(): lax.all_gather(conditioned, ('row', 'col'), axis=1, tiled=True)  18.6 us
    all_gather x1, blocking collectives, on_device(): lax.all_gather(flattened, 'row', axis=1, tiled=True)  9.09 us
  transfers between devices with their start and end apart: 4, of which 4 were waited for; matrix products, arithmetic and copies ran while one was open for 0% of the time, Pallas kernels for 0%

commit v1 on v0

v1 whole, which is shorter than its diff:
```python
import functools

import jax
import jax.numpy as jnp
from jax import lax
from jax.experimental import pallas as pl
from jax.experimental.pallas import tpu as pltpu
from jax.sharding import PartitionSpec as P

F32 = jnp.float32
BF16 = jnp.bfloat16
AXES = ("row", "col", "store")
NT = (((1,), (1,)), ((), ()))
NN = (((1,), (0,)), ((), ()))
VMEM = pl.BlockSpec(memory_space=pltpu.VMEM)
SMEM = pl.BlockSpec(memory_space=pltpu.SMEM)


def dot(a, b, dims):
    return lax.dot_general(a, b, dims, preferred_element_type=F32)


def project_kernel(n_col, lengths, hidden, proj_in_t, grads, proj_out, out, grads_f32, weights):
    dest = pl.program_id(0)
    rows, queries, tokens = grads.shape
    q_dest, t_part, columns = hidden.shape
    width = proj_out.shape[1]

    @pl.when(dest == 0)
    def _():
        grads_f32[...] = grads[...].astype(F32).reshape(rows * queries, tokens)
        i = lax.broadcasted_iota(jnp.int32, (width, width), 0)
        j = lax.broadcasted_iota(jnp.int32, (width, width), 1)
        half = width // 2
        pick = j == jnp.where(i < half, 2 * i, 2 * (i - half) + 1)
        weights[...] = dot(pick.astype(BF16), proj_out[...], NT).astype(BF16)

    v = dot(proj_in_t[...], hidden[...].reshape(q_dest * t_part, columns), NT)
    width_in = v.shape[0]
    out[0, 0:width_in, :] = v.astype(BF16)
    share = q_dest // n_col
    lane = lax.broadcasted_iota(jnp.int32, (width, tokens), 1)
    for i in range(share):
        q = dest * q_dest + lax.axis_index("col") * share + i
        g = grads_f32[pl.ds(q, rows, stride=queries), :].astype(BF16)
        u = dot(weights[...], g, NN)
        u = jnp.where(lane < lengths[q], u, 0.0)
        at = width_in + i * width
        out[0, at : at + width, :] = u.astype(BF16)


def feature_kernel(n_row, n_col, q_dest, width, width_in, copies, got, out, held):
    tokens = got.shape[2]
    t_part = tokens // q_dest
    share = q_dest // n_col
    half = width // 2
    scale = tokens ** (-0.5)
    lane_v = lax.broadcasted_iota(jnp.int32, (width_in, tokens), 1)
    parts = [[got[b * n_col + c, 0:width_in, :].astype(F32) for b in range(n_row)] for c in range(n_col)]
    lane_f = lax.broadcasted_iota(jnp.int32, (half, n_col * width_in), 1)
    for q in range(q_dest):
        v_rows = []
        for c in range(n_col):
            v = None
            for b in range(n_row):
                shift = ((b - q) * t_part) % tokens
                part = pltpu.roll(parts[c][b], shift, 1) if shift else parts[c][b]
                v = part if v is None else jnp.where(lane_v >= b * t_part, part, v)
            v_rows.append(v)
        v_all = jnp.concatenate(v_rows, axis=0).astype(BF16)
        at = width_in + (q % share) * width
        total = None
        for b in range(n_row):
            u = got[b * n_col + q // share, at : at + width, :]
            term = dot(u, v_all, NT)
            total = term if total is None else total + term
        total = total + pltpu.roll(total, width_in, 1)
        packed = jnp.where(lane_f < width_in, total[:half], total[half:]) * scale
        held[pl.ds(q, half, stride=q_dest), :] = packed
    n = held.shape[0] // n_row
    for r in range(n_row):
        block = held[r * n : (r + 1) * n, :].astype(BF16)
        for k in range(copies):
            out[r * copies + k] = block


def condition_kernel(n_row, n_col, q_dest, got, p_own, p_got, keep, send, got_f32):
    sources, rows, lanes = got.shape
    got_f32[...] = got[...].astype(F32).reshape(sources * rows, lanes)
    col = lax.axis_index("col")
    core = lax.rem(lax.axis_index("row"), 2)
    pairs = rows // q_dest
    here = pairs // n_col
    depth, width = p_got.shape
    mine = pl.ds(pl.multiple_of(col * width, width), width)

    def features(side, half):
        columns = []
        for i in range(here):
            blocks = []
            for h in range(q_dest // 2):
                at = (half * here + i) * q_dest + 2 * h + side
                blocks.append(got_f32[pl.ds(at, sources, stride=rows), :])
            columns.append(jnp.concatenate(blocks, axis=0).astype(BF16))
        return jnp.concatenate(columns, axis=1)

    for ref, side in ((send, 1 - core), (keep, core)):
        acc = dot(features(side, col), p_own[:, mine], NN)
        acc += dot(features(side, 1 - col), p_got[...], NN)
        ref[...] = acc.reshape(ref.shape)


def fold_kernel(keep, got, mine, other):
    x = lax.axis_index("row") // 2
    other[...] = keep[1 - x] + got[1 - x]
    mine[...] = keep[x] + got[x]


def finish_kernel(mine, got, out):
    out[...] = (mine[...] + got[...]).astype(BF16)


def score_kernel(n_row, n_col, n_store, q_dest, near, far, stored, out, held, ordered):
    sources, width = near.shape[2:]
    row, col, store = (lax.axis_index(a) for a in AXES)
    x, core = row // 2, lax.rem(row, 2)
    n_x = n_row // 2
    acc = None
    for iy in range(n_col):
        for iz in range(n_store):
            y, z = lax.bitwise_xor(col, iy), lax.bitwise_xor(store, iz)
            at = pl.multiple_of((z * n_col + y) * width, width)
            left = jnp.concatenate([ref[ix * n_col + iy, iz] for ref in (near, far) for ix in range(n_x)], axis=0)
            term = dot(left, stored[:, pl.ds(at, width)], NT)
            acc = term if acc is None else acc + term
    lanes = held.shape[2]
    for i in range(held.shape[0]):
        held[i] = acc[:, i * lanes : (i + 1) * lanes]
    group = n_row * n_col
    for i in range(held.shape[0]):
        for side in range(2):
            for ix in range(n_x):
                q4 = lax.bitwise_xor(x, ix) * 2 + lax.bitwise_xor(core, side)
                base = (side * n_x + ix) * sources
                for s in range(n_store):
                    rows = held[i, pl.ds(base + s, group, stride=n_store), :]
                    ordered[i, pl.ds(s * group * q_dest + q4, group, stride=q_dest), :] = rows
        out[:, i * lanes : (i + 1) * lanes] = ordered[i]


def call(kernel, outs, in_specs, scratch=(), flops=0, size=0, **more):
    return pl.pallas_call(
        kernel,
        out_shape=outs,
        in_specs=in_specs,
        scratch_shapes=list(scratch),
        cost_estimate=pl.CostEstimate(flops=flops, bytes_accessed=size, transcendentals=0),
        **more,
    )


def shape(s, t):
    return jax.ShapeDtypeStruct(s, t)


def swap(x, axis, n, k):
    return lax.ppermute(x, axis, [(i, i ^ k) for i in range(n)])


def split_device(sizes, hidden, out_grads, proj_out, proj_in, lengths, precond, stored):
    n_row, n_col, n_store = sizes
    group = n_row * n_col
    queries, t_part, columns = hidden.shape
    rows, _, tokens = out_grads.shape
    width, width_in = proj_out.shape[1], proj_in.shape[1]
    q_dest = queries // group
    share = q_dest // n_col
    depth = width_in + share * width
    col = lax.axis_index("col")
    j_width = precond.shape[1] // n_col

    p_send = lax.dynamic_slice_in_dim(precond, (1 - col) * j_width, j_width, axis=1)
    p_got = swap(p_send, "col", n_col, 1)

    const = lambda nd: (lambda i: (0,) * nd)
    blocks = pl.pallas_call(
        functools.partial(project_kernel, n_col),
        grid=(group,),
        in_specs=[
            SMEM,
            pl.BlockSpec((q_dest, t_part, columns), lambda i: (i, 0, 0)),
            pl.BlockSpec((width_in, columns), const(2)),
            pl.BlockSpec(out_grads.shape, const(3)),
            pl.BlockSpec(proj_out.shape, const(2)),
        ],
        out_specs=pl.BlockSpec((1, depth, tokens), lambda i: (i, 0, 0)),
        out_shape=shape((group, depth, tokens), BF16),
        scratch_shapes=[pltpu.VMEM((rows * queries, tokens), F32), pltpu.VMEM((width, rows), BF16)],
        cost_estimate=pl.CostEstimate(flops=2 * hidden.size * width_in, bytes_accessed=2 * hidden.size, transcendentals=0),
    )(lengths, hidden, proj_in.T, out_grads, proj_out)
    got = lax.all_to_all(blocks, ("row", "col"), 0, 0)

    copies = n_col * n_store
    half = width // 2
    n = half * q_dest // n_row
    feats = call(
        functools.partial(feature_kernel, n_row, n_col, q_dest, width, width_in, copies),
        shape((n_row * copies, n, tokens), BF16),
        [VMEM],
        [pltpu.VMEM((half * q_dest, tokens), F32)],
        size=2 * got.size,
    )(got)
    feats = lax.all_to_all(feats, AXES, 0, 0)

    sources = group * n_store
    part = shape((q_dest // 2, sources, j_width), F32)
    keep, send = call(
        functools.partial(condition_kernel, n_row, n_col, q_dest),
        (part, part),
        [VMEM, VMEM, VMEM],
        [pltpu.VMEM((sources * n, tokens), F32)],
        size=2 * precond.size,
    )(feats, precond, p_got)
    got = swap(send, "row", n_row, 1)
    piece = shape((sources, j_width), F32)
    mine, other = call(fold_kernel, (piece, piece), [VMEM, VMEM], size=keep.size * 8)(keep, got)
    got = swap(other, "row", n_row, 2)
    cond = call(finish_kernel, shape(piece.shape, BF16), [VMEM, VMEM], size=mine.size * 8)(mine, got)

    cond = jnp.stack([cond] + [swap(cond, "store", n_store, k) for k in range(1, n_store)])
    pairs = lambda a, k: [(i, i ^ k) for i in range(a)]
    diag = [(r * n_col + c, (r ^ 2) * n_col + (c ^ 1)) for r in range(n_row) for c in range(n_col)]
    near = jnp.stack(
        [
            cond,
            swap(cond, "col", n_col, 1),
            swap(cond, "row", n_row, 2),
            lax.ppermute(cond, ("row", "col"), diag),
        ]
    )
    far = swap(near, "row", n_row, 1)
    return call(
        functools.partial(score_kernel, n_row, n_col, n_store, q_dest),
        shape((sources * q_dest, stored.shape[0]), F32),
        [VMEM, VMEM, VMEM],
        [pltpu.VMEM((stored.shape[0] // 128, sources * q_dest, 128), F32)] * 2,
        size=2 * stored.size,
    )(near, far, stored)


def plain_device(hidden, out_grads, proj_out, proj_in, lengths, precond, stored):
    queries, token_part, columns = hidden.shape
    width_in = proj_in.shape[1]
    local_proj = jnp.einsum("qtc,cb->qtb", hidden, proj_in, preferred_element_type=F32).astype(BF16)
    flattened = local_proj.reshape(queries, token_part * width_in)
    inputs_all = lax.all_gather(flattened, "row", axis=1, tiled=True).reshape(queries, -1, width_in)
    tokens = inputs_all.shape[1]
    position = jnp.arange(tokens, dtype=jnp.int32)
    live_mask = (position[None, :] < lengths[:, None]).astype(F32)
    outputs_proj = jnp.einsum("rqt,ra->qta", out_grads, proj_out, preferred_element_type=F32)
    outputs_proj = (outputs_proj * live_mask[:, :, None]).astype(BF16)
    partial_value = jnp.einsum("qta,qtb->qab", outputs_proj, inputs_all, preferred_element_type=F32)
    partial_value = partial_value.reshape(queries, -1) * tokens ** (-0.5)
    shares = lax.psum_scatter(partial_value, ("row", "col"), scatter_dimension=1, tiled=True).astype(BF16)
    cond_terms = jnp.dot(shares, lax.all_gather(precond, "store", axis=1, tiled=True), preferred_element_type=F32)
    conditioned = lax.psum_scatter(cond_terms, ("row", "col"), scatter_dimension=1, tiled=True).astype(BF16)
    full_features = lax.all_gather(conditioned, ("row", "col"), axis=1, tiled=True)
    return lax.dot_general(
        lax.all_gather(full_features, "store", axis=0, tiled=True),
        stored,
        NT,
        preferred_element_type=F32,
    )


def solution(mesh):
    sizes = tuple(mesh.shape[a] for a in AXES)
    group = sizes[0] * sizes[1]

    def on_device(hidden, out_grads, proj_out, proj_in, lengths, precond, stored):
        args = (hidden, out_grads, proj_out, proj_in, lengths, precond, stored)
        queries = hidden.shape[0]
        fits = sizes[0] == 4 and sizes[1] == 2 and sizes[2] & (sizes[2] - 1) == 0
        fits = fits and queries % group == 0 and queries // group == sizes[0]
        fits = fits and proj_in.shape[1] * sizes[1] == 128 and proj_out.shape[1] * 2 == 128
        fits = fits and stored.shape[0] % 128 == 0 and out_grads.shape[2] == 128 and queries // group * hidden.shape[1] == 128
        if fits:
            return split_device(sizes, *args)
        return plain_device(*args)

    return jax.shard_map(
        on_device,
        mesh=mesh,
        in_specs=(
            P("store", "row", "col"),
            P("row", "store", None),
            P("row", None),
            P("col", None),
            P("store"),
            P(("row", "col"), "store"),
            P(("row", "col", "store"), None),
        ),
        out_specs=P(None, ("row", "col", "store")),
        check_vma=False,
    )
```

time: 208 us -> 74.8 us (0.36)
  waiting for transfers between devices: 144 us -> 29 us
  blocking collectives: 27.7 us -> 0 us
  starting transfers between devices: 0.13 us -> 21.2 us
  Pallas kernels: 0 us -> 19.5 us
  between operations: 14.9 us -> 0.06 us
  matrix products: 13.4 us -> 0 us
    all_gather x2 -> x0, waiting for transfers between devices: 76.4 us -> none  [the longest x1 48.4 us: on_device(): lax.all_gather(precond, 'store', axis=1, tiled=True)]
    reduce_scatter x2 -> x0, waiting for transfers between devices: 67.2 us -> none  [the longest x1 34.5 us: on_device(): lax.psum_scatter(partial_value, ('row', 'col'), scatter_dimension=1, tile...]
    all_gather x2 -> x0, blocking collectives: 27.7 us -> none  [the longest x1 18.6 us: on_device(): lax.all_gather(conditioned, ('row', 'col'), axis=1, tiled=True)]
    pallas_call x0 -> x6, Pallas kernels: none -> 19.5 us  [the longest x1 7.36 us: split_device(): pl.pallas_call(functools.partial(project_kernel, n_col), grid=(group,), i...]
    ppermute x0 -> x10, waiting for transfers between devices: none -> 16.5 us  [the longest x9 14.9 us: swap(): return lax.ppermute(x, axis, [(i, i ^ k) for i in range(n)])]
    dot_general x4 -> x0, matrix products: 13.4 us -> none  [the longest x1 3.87 us: on_device(): jnp.dot(shares, lax.all_gather(precond, 'store', axis=1, tiled=True), pre...]
    all_to_all x0 -> x2, waiting for transfers between devices: none -> 12.6 us  [the longest x1 7.31 us: split_device(): feats = lax.all_to_all(feats, AXES, 0, 0)]
    ppermute x0 -> x10, starting transfers between devices: none -> 11.1 us  [the longest x9 9.23 us: swap(): return lax.ppermute(x, axis, [(i, i ^ k) for i in range(n)])]
  transfers between devices with their start and end apart: 4 -> 12, of which waited for: 4 -> 11; matrix products, arithmetic and copies ran while one was open for 0% -> 0% of each run, Pallas kernels for 0% -> 3%
where the time goes in v1:
time: 74.8 us; the launch traced here: 74.2 us
  waiting for transfers between devices  29 us (39%)
  starting transfers between devices  21.2 us (28%)
  Pallas kernels  19.5 us (26%)
  local copies, waits for them, and re-layouts  3.59 us (5%)
  other arithmetic  0.85 us (1%)
    ppermute x9, waiting for transfers between devices, swap(): return lax.ppermute(x, axis, [(i, i ^ k) for i in range(n)])  14.9 us
    ppermute x9, starting transfers between devices, swap(): return lax.ppermute(x, axis, [(i, i ^ k) for i in range(n)])  9.23 us
    pallas_call x1, Pallas kernels, split_device(): pl.pallas_call(functools.partial(project_kernel, n_col), grid=(group,), i...  7.36 us
    all_to_all x1, waiting for transfers between devices, split_device(): feats = lax.all_to_all(feats, AXES, 0, 0)  7.31 us
    all_to_all x1, waiting for transfers between devices, split_device(): got = lax.all_to_all(blocks, ('row', 'col'), 0, 0)  5.28 us
    all_to_all x1, starting transfers between devices, split_device(): got = lax.all_to_all(blocks, ('row', 'col'), 0, 0)  5.21 us
    all_to_all x1, starting transfers between devices, split_device(): feats = lax.all_to_all(feats, AXES, 0, 0)  4.87 us
    pallas_call x1, Pallas kernels, split_device(): call(functools.partial(score_kernel, n_row, n_col, n_store, q_dest), shap...  4 us
  transfers between devices with their start and end apart: 12, of which 11 were waited for; matrix products, arithmetic and copies ran while one was open for 0% of the time, Pallas kernels for 3%

profile of v1, /device:TPU:0, one launch (start us, length us, event | category | flops | bytes accessed | tf_op | source)
XLA Modules:
  0.0 74.2 jit_solution(155719600689617719)
XLA Ops:
  0.0 7.4 %shard_map.73 = bf16[8,192,128]{2,1,0:T(8,128)(2,1)} custom-call(s32[32]{0:T(128)} %lengths.1, bf16[32,32,2048]{2,1,0:T(8,128)(2,1)} %hidden.1, bf16[64,2048]{1,0:T(8,128)(2,1)} %bitcast.10, bf16[52,32,128]{2,1,0:T(8,128)(2,1)} %grads.1, bf16[52,64]{1,0:T(8,128)(2,1)} %proj_out.1), custom_call_target="tpu_custom_call" | custom-call | flops 268435456 | bytes 4194304 | tf_op jit(solution)/shard_map/pallas_call | solution.py:186
  7.4 5.2 %all-to-all-start = ((bf16[8,192,128]{2,1,0:T(8,128)(2,1)}), bf16[8,192,128]{2,1,0:T(8,128)(2,1)S(1)}, u32[]{:S(2)}, u32[]{:S(2)}) async-start(bf16[8,192,128]{2,1,0:T(8,128)(2,1)} %shard_map.73), calls=%async_computation | async-start | bytes 786432 | tf_op jit(solution)/shard_map/all_to_all | solution.py:201
  12.6 2.1 %collective-permute-start = (bf16[512,512]{1,0:T(8,128)(2,1)S(1)}, bf16[512,512]{1,0:T(8,128)(2,1)S(1)}, u32[]{:S(2)}, u32[]{:S(2)}) collective-permute-start(bf16[512,512]{1,0:T(8,128)(2,1)S(1)} %constant_dynamic-slice_fusion), channel_id=1, source_target_pairs={{0,4},{4,0},{1,5},{5,1},{2,6},{6,2},{3,7},{7,3},{8,12},{12,8},{9,1... | collective-permute-start | bytes 1572872 | tf_op jit(solution)/shard_map/ppermute | solution.py:167
  14.7 5.3 %all-to-all-done.got = bf16[8,192,128]{2,1,0:T(8,128)(2,1)S(1)} async-done(((bf16[8,192,128]{2,1,0:T(8,128)(2,1)}), bf16[8,192,128]{2,1,0:T(8,128)(2,1)S(1)}, u32[]{:S(2)}, u32[]{:S(2)}) %all-to-all-start) | async-done | bytes 393248 | tf_op jit(solution)/shard_map/all_to_all | solution.py:201
  20.7 2.3 %shard_map.74 = bf16[32,32,128]{2,1,0:T(8,128)(2,1)} custom-call(bf16[8,192,128]{2,1,0:T(8,128)(2,1)} %copy-done.2), custom_call_target="tpu_custom_call" | custom-call | bytes 393216 | tf_op jit(solution)/shard_map/pallas_call | solution.py:206
  23.1 4.9 %all-to-all-start.1 = ((bf16[32,32,128]{2,1,0:T(8,128)(2,1)}), bf16[32,32,128]{2,1,0:T(8,128)(2,1)S(1)}, u32[]{:S(2)}, u32[]{:S(2)}) async-start(bf16[32,32,128]{2,1,0:T(8,128)(2,1)} %shard_map.74), calls=%async_computation.1 | async-start | bytes 524288 | tf_op jit(solution)/shard_map/all_to_all | solution.py:213
  27.9 3.4 %collective-permute-done.p_got = bf16[512,512]{1,0:T(8,128)(2,1)S(1)} collective-permute-done((bf16[512,512]{1,0:T(8,128)(2,1)S(1)}, bf16[512,512]{1,0:T(8,128)(2,1)S(1)}, u32[]{:S(2)}, u32[]{:S(2)}) %collective-permute-start) | collective-permute-done | bytes 524320 | tf_op jit(solution)/shard_map/ppermute | solution.py:167
  31.4 7.3 %all-to-all-done.1.got = bf16[32,32,128]{2,1,0:T(8,128)(2,1)S(1)} async-done(((bf16[32,32,128]{2,1,0:T(8,128)(2,1)}), bf16[32,32,128]{2,1,0:T(8,128)(2,1)S(1)}, u32[]{:S(2)}, u32[]{:S(2)}) %all-to-all-start.1) | async-done | bytes 262176 | tf_op jit(solution)/shard_map/all_to_all | solution.py:213
  39.4 2.7 %shard_map.75 = (f32[2,32,512]{2,1,0:T(8,128)}, f32[2,32,512]{2,1,0:T(8,128)}) custom-call(bf16[32,32,128]{2,1,0:T(8,128)(2,1)} %copy-done.3, bf16[512,1024]{1,0:T(8,128)(2,1)} %p_own.1, bf16[512,512]{1,0:T(8,128)(2,1)} %copy-done.4), custom_call_target="tpu_custom_call" | custom-call | bytes 1048576 | tf_op jit(solution)/shard_map/pallas_call | solution.py:217
  42.2 1.4 %collective-permute-done.1.got = f32[2,32,512]{2,1,0:T(8,128)S(1)} collective-permute-done((f32[2,32,512]{2,1,0:T(8,128)}, f32[2,32,512]{2,1,0:T(8,128)S(1)}, u32[]{:S(2)}, u32[]{:S(2)}) %collective-permute-start.1) | collective-permute-done | bytes 131104 | tf_op jit(solution)/shard_map/ppermute | solution.py:167
  44.3 1.6 %shard_map.76 = (f32[32,512]{1,0:T(8,128)}, f32[32,512]{1,0:T(8,128)}) custom-call(f32[2,32,512]{2,1,0:T(8,128)} %get-tuple-element.9.keep, f32[2,32,512]{2,1,0:T(8,128)} %copy-done.6), custom_call_target="tpu_custom_call" | custom-call | bytes 262144 | tf_op jit(solution)/shard_map/pallas_call | solution.py:226
  45.9 0.9 %collective-permute-start.2 = (f32[32,512]{1,0:T(8,128)}, f32[32,512]{1,0:T(8,128)S(1)}, u32[]{:S(2)}, u32[]{:S(2)}) collective-permute-start(f32[32,512]{1,0:T(8,128)} %get-tuple-element.12), channel_id=1, source_target_pairs={{0,16},{8,24},{16,0},{24,8},{1,17},{9,25},{17,1},{25,9},{2,18},{10... | collective-permute-start | bytes 196616 | tf_op jit(solution)/shard_map/ppermute | solution.py:167
  46.8 3.6 %collective-permute-done.2.got = f32[32,512]{1,0:T(8,128)S(1)} collective-permute-done((f32[32,512]{1,0:T(8,128)}, f32[32,512]{1,0:T(8,128)S(1)}, u32[]{:S(2)}, u32[]{:S(2)}) %collective-permute-start.2) | collective-permute-done | bytes 65568 | tf_op jit(solution)/shard_map/ppermute | solution.py:167
  51.0 1.5 %shard_map.77 = bf16[32,512]{1,0:T(8,128)(2,1)} custom-call(f32[32,512]{1,0:T(8,128)} %get-tuple-element.11.mine, f32[32,512]{1,0:T(8,128)} %copy-done.7), custom_call_target="tpu_custom_call" | custom-call | bytes 131072 | tf_op jit(solution)/shard_map/pallas_call | solution.py:228
  53.1 1.0 %collective-permute-start.4 = (bf16[32,512]{1,0:T(8,128)(2,1)}, bf16[32,512]{1,0:T(8,128)(2,1)S(1)}, u32[]{:S(2)}, u32[]{:S(2)}) collective-permute-start(bf16[32,512]{1,0:T(8,128)(2,1)} %shard_map.77), channel_id=1, source_target_pairs={{0,2},{1,3},{2,0},{3,1},{4,6},{5,7},{6,4},{7,5},{8,10},{9,11},{10,... | collective-permute-start | bytes 98312 | tf_op jit(solution)/shard_map/ppermute | solution.py:167
  54.2 2.7 %collective-permute-start.3 = (bf16[32,512]{1,0:T(8,128)(2,1)}, bf16[32,512]{1,0:T(8,128)(2,1)S(1)}, u32[]{:S(2)}, u32[]{:S(2)}) collective-permute-start(bf16[32,512]{1,0:T(8,128)(2,1)} %shard_map.77), channel_id=1, source_target_pairs={{0,1},{1,0},{2,3},{3,2},{4,5},{5,4},{6,7},{7,6},{8,9},{9,8},{10,11... | collective-permute-start | bytes 98312 | tf_op jit(solution)/shard_map/ppermute | solution.py:167
  56.9 1.6 %collective-permute-done.5 = bf16[32,512]{1,0:T(8,128)(2,1)S(1)} collective-permute-done((bf16[32,512]{1,0:T(8,128)(2,1)}, bf16[32,512]{1,0:T(8,128)(2,1)S(1)}, u32[]{:S(2)}, u32[]{:S(2)}) %collective-permute-start.5) | collective-permute-done | bytes 32800 | tf_op jit(solution)/shard_map/ppermute | solution.py:167
  59.8 1.0 %collective-permute-start.7 = (bf16[4,32,512]{2,1,0:T(8,128)(2,1)S(1)}, bf16[4,32,512]{2,1,0:T(8,128)(2,1)S(1)}, u32[]{:S(2)}, u32[]{:S(2)}) collective-permute-start(bf16[4,32,512]{2,1,0:T(8,128)(2,1)S(1)} %get-tuple-element.14), channel_id=1, source_target_pairs={{0,16},{8,24},{16,0},{24,8},{1,17},{9,25},{17,1},{25,9},{2,18},{10... | collective-permute-start | bytes 393224 | tf_op jit(solution)/shard_map/ppermute | solution.py:167
  61.5 1.9 %collective-permute-start.8 = (bf16[4,32,512]{2,1,0:T(8,128)(2,1)S(1)}, bf16[4,32,512]{2,1,0:T(8,128)(2,1)S(1)}, u32[]{:S(2)}, u32[]{:S(2)}) collective-permute-start(bf16[4,32,512]{2,1,0:T(8,128)(2,1)S(1)} %get-tuple-element.14), channel_id=1, source_target_pairs={{0,20},{4,16},{8,28},{12,24},{16,4},{20,0},{24,12},{28,8},{1,21},{... | collective-permute-start | bytes 393224 | tf_op jit(solution)/shard_map/ppermute | solution.py:238
  63.4 1.5 %collective-permute-done.7 = bf16[4,32,512]{2,1,0:T(8,128)(2,1)S(1)} collective-permute-done((bf16[4,32,512]{2,1,0:T(8,128)(2,1)S(1)}, bf16[4,32,512]{2,1,0:T(8,128)(2,1)S(1)}, u32[]{:S(2)}, u32[]{:S(2)}) %collective-permute-start.7) | collective-permute-done | bytes 131104 | tf_op jit(solution)/shard_map/ppermute | solution.py:167
  64.8 0.9 %collective-permute-done.6 = bf16[4,32,512]{2,1,0:T(8,128)(2,1)S(1)} collective-permute-done((bf16[4,32,512]{2,1,0:T(8,128)(2,1)S(1)}, bf16[4,32,512]{2,1,0:T(8,128)(2,1)S(1)}, u32[]{:S(2)}, u32[]{:S(2)}) %collective-permute-start.6) | collective-permute-done | bytes 131104 | tf_op jit(solution)/shard_map/ppermute | solution.py:167
  65.8 1.6 %collective-permute-done.8 = bf16[4,32,512]{2,1,0:T(8,128)(2,1)S(1)} collective-permute-done((bf16[4,32,512]{2,1,0:T(8,128)(2,1)S(1)}, bf16[4,32,512]{2,1,0:T(8,128)(2,1)S(1)}, u32[]{:S(2)}, u32[]{:S(2)}) %collective-permute-start.8) | collective-permute-done | bytes 131104 | tf_op jit(solution)/shard_map/ppermute | solution.py:238
  67.5 1.9 %collective-permute-done.9.far = bf16[4,4,32,512]{3,2,1,0:T(8,128)(2,1)S(1)} collective-permute-done((bf16[4,4,32,512]{3,2,1,0:T(8,128)(2,1)S(1)}, bf16[4,4,32,512]{3,2,1,0:T(8,128)(2,1)S(1)}, u32[]{:S(2)}, u32[]{:S(2)}) %collective-permute-start.9) | collective-permute-done | bytes 524320 | tf_op jit(solution)/shard_map/ppermute | solution.py:167
  70.2 4.0 %shard_map.78 = f32[128,384]{1,0:T(8,128)} custom-call(bf16[4,4,32,512]{3,2,1,0:T(8,128)(2,1)} %copy-done.1, bf16[4,4,32,512]{3,2,1,0:T(8,128)(2,1)} %copy-done.5, bf16[384,4096]{1,0:T(8,128)(2,1)} %stored.1), custom_call_target="tpu_custom_call" | custom-call | bytes 3145728 | tf_op jit(solution)/shard_map/pallas_call | solution.py:242
  (25 shorter events, 6.5 us)
Async XLA Ops:
  0.0 12.6 %copy-start = (bf16[512,1024]{1,0:T(8,128)(2,1)S(1)}, bf16[512,1024]{1,0:T(8,128)(2,1)}, u32[]{:S(2)}) copy-start(bf16[512,1024]{1,0:T(8,128)(2,1)} %p_own.1) | copy-start | bytes 3145732
  7.4 12.6 %all-to-all-start = ((bf16[8,192,128]{2,1,0:T(8,128)(2,1)}), bf16[8,192,128]{2,1,0:T(8,128)(2,1)S(1)}, u32[]{:S(2)}, u32[]{:S(2)}) async-start(bf16[8,192,128]{2,1,0:T(8,128)(2,1)} %shard_map.73), calls=%async_computation | async-start | bytes 786432 | tf_op jit(solution)/shard_map/all_to_all | solution.py:201
  12.6 18.8 %collective-permute-start = (bf16[512,512]{1,0:T(8,128)(2,1)S(1)}, bf16[512,512]{1,0:T(8,128)(2,1)S(1)}, u32[]{:S(2)}, u32[]{:S(2)}) collective-permute-start(bf16[512,512]{1,0:T(8,128)(2,1)S(1)} %constant_dynamic-slice_fusion), channel_id=1, source_target_pairs={{0,4},{4,0},{1,5},{5,1},{2,6},{6,2},{3,7},{7,3},{8,12},{12,8},{9,1... | collective-permute-start | bytes 1572872 | tf_op jit(solution)/shard_map/ppermute | solution.py:167
  20.0 0.8 %copy-start.2 = (bf16[8,192,128]{2,1,0:T(8,128)(2,1)}, bf16[8,192,128]{2,1,0:T(8,128)(2,1)S(1)}, u32[]{:S(2)}) copy-start(bf16[8,192,128]{2,1,0:T(8,128)(2,1)S(1)} %all-to-all-done.got) | copy-start | bytes 1179652
  23.1 15.6 %all-to-all-start.1 = ((bf16[32,32,128]{2,1,0:T(8,128)(2,1)}), bf16[32,32,128]{2,1,0:T(8,128)(2,1)S(1)}, u32[]{:S(2)}, u32[]{:S(2)}) async-start(bf16[32,32,128]{2,1,0:T(8,128)(2,1)} %shard_map.74), calls=%async_computation.1 | async-start | bytes 524288 | tf_op jit(solution)/shard_map/all_to_all | solution.py:213
  31.4 7.3 %copy-start.4 = (bf16[512,512]{1,0:T(8,128)(2,1)}, bf16[512,512]{1,0:T(8,128)(2,1)S(1)}, u32[]{:S(2)}) copy-start(bf16[512,512]{1,0:T(8,128)(2,1)S(1)} %collective-permute-done.p_got) | copy-start | bytes 1572868
  38.7 0.7 copy-start.3
  42.1 1.6 %collective-permute-start.1 = (f32[2,32,512]{2,1,0:T(8,128)}, f32[2,32,512]{2,1,0:T(8,128)S(1)}, u32[]{:S(2)}, u32[]{:S(2)}) collective-permute-start(f32[2,32,512]{2,1,0:T(8,128)} %get-tuple-element.10), channel_id=1, source_target_pairs={{0,8},{8,0},{16,24},{24,16},{1,9},{9,1},{17,25},{25,17},{2,10},{10... | collective-permute-start | bytes 393224 | tf_op jit(solution)/shard_map/ppermute | solution.py:167
  43.6 0.6 copy-start.6
  45.9 4.5 %collective-permute-start.2 = (f32[32,512]{1,0:T(8,128)}, f32[32,512]{1,0:T(8,128)S(1)}, u32[]{:S(2)}, u32[]{:S(2)}) collective-permute-start(f32[32,512]{1,0:T(8,128)} %get-tuple-element.12), channel_id=1, source_target_pairs={{0,16},{8,24},{16,0},{24,8},{1,17},{9,25},{17,1},{25,9},{2,18},{10... | collective-permute-start | bytes 196616 | tf_op jit(solution)/shard_map/ppermute | solution.py:167
  50.4 0.6 copy-start.7
  52.5 6.0 %collective-permute-start.5 = (bf16[32,512]{1,0:T(8,128)(2,1)}, bf16[32,512]{1,0:T(8,128)(2,1)S(1)}, u32[]{:S(2)}, u32[]{:S(2)}) collective-permute-start(bf16[32,512]{1,0:T(8,128)(2,1)} %shard_map.77), channel_id=1, source_target_pairs={{0,3},{1,2},{2,1},{3,0},{4,7},{5,6},{6,5},{7,4},{8,11},{9,10},{10,... | collective-permute-start | bytes 98312 | tf_op jit(solution)/shard_map/ppermute | solution.py:167
  53.1 5.4 %collective-permute-start.4 = (bf16[32,512]{1,0:T(8,128)(2,1)}, bf16[32,512]{1,0:T(8,128)(2,1)S(1)}, u32[]{:S(2)}, u32[]{:S(2)}) collective-permute-start(bf16[32,512]{1,0:T(8,128)(2,1)} %shard_map.77), channel_id=1, source_target_pairs={{0,2},{1,3},{2,0},{3,1},{4,6},{5,7},{6,4},{7,5},{8,10},{9,11},{10,... | collective-permute-start | bytes 98312 | tf_op jit(solution)/shard_map/ppermute | solution.py:167
  54.2 4.9 %collective-permute-start.3 = (bf16[32,512]{1,0:T(8,128)(2,1)}, bf16[32,512]{1,0:T(8,128)(2,1)S(1)}, u32[]{:S(2)}, u32[]{:S(2)}) collective-permute-start(bf16[32,512]{1,0:T(8,128)(2,1)} %shard_map.77), channel_id=1, source_target_pairs={{0,1},{1,0},{2,3},{3,2},{4,5},{5,4},{6,7},{7,6},{8,9},{9,8},{10,11... | collective-permute-start | bytes 98312 | tf_op jit(solution)/shard_map/ppermute | solution.py:167
  59.8 5.0 %collective-permute-start.7 = (bf16[4,32,512]{2,1,0:T(8,128)(2,1)S(1)}, bf16[4,32,512]{2,1,0:T(8,128)(2,1)S(1)}, u32[]{:S(2)}, u32[]{:S(2)}) collective-permute-start(bf16[4,32,512]{2,1,0:T(8,128)(2,1)S(1)} %get-tuple-element.14), channel_id=1, source_target_pairs={{0,16},{8,24},{16,0},{24,8},{1,17},{9,25},{17,1},{25,9},{2,18},{10... | collective-permute-start | bytes 393224 | tf_op jit(solution)/shard_map/ppermute | solution.py:167
  60.8 5.0 %collective-permute-start.6 = (bf16[4,32,512]{2,1,0:T(8,128)(2,1)S(1)}, bf16[4,32,512]{2,1,0:T(8,128)(2,1)S(1)}, u32[]{:S(2)}, u32[]{:S(2)}) collective-permute-start(bf16[4,32,512]{2,1,0:T(8,128)(2,1)S(1)} %get-tuple-element.14), channel_id=1, source_target_pairs={{0,4},{4,0},{1,5},{5,1},{2,6},{6,2},{3,7},{7,3},{8,12},{12,8},{9,1... | collective-permute-start | bytes 393224 | tf_op jit(solution)/shard_map/ppermute | solution.py:167
  61.5 5.9 %collective-permute-start.8 = (bf16[4,32,512]{2,1,0:T(8,128)(2,1)S(1)}, bf16[4,32,512]{2,1,0:T(8,128)(2,1)S(1)}, u32[]{:S(2)}, u32[]{:S(2)}) collective-permute-start(bf16[4,32,512]{2,1,0:T(8,128)(2,1)S(1)} %get-tuple-element.14), channel_id=1, source_target_pairs={{0,20},{4,16},{8,28},{12,24},{16,4},{20,0},{24,12},{28,8},{1,21},{... | collective-permute-start | bytes 393224 | tf_op jit(solution)/shard_map/ppermute | solution.py:238
  67.4 2.0 %copy-start.1 = (bf16[4,4,32,512]{3,2,1,0:T(8,128)(2,1)}, bf16[4,4,32,512]{3,2,1,0:T(8,128)(2,1)S(1)}, u32[]{:S(2)}) copy-start(bf16[4,4,32,512]{3,2,1,0:T(8,128)(2,1)S(1)} %pad_maximum_fusion.near) | copy-start | bytes 1572868
  67.4 2.0 %collective-permute-start.9 = (bf16[4,4,32,512]{3,2,1,0:T(8,128)(2,1)S(1)}, bf16[4,4,32,512]{3,2,1,0:T(8,128)(2,1)S(1)}, u32[]{:S(2)}, u32[]{:S(2)}) collective-permute-start(bf16[4,4,32,512]{3,2,1,0:T(8,128)(2,1)S(1)} %pad_maximum_fusion.near), channel_id=1, source_target_pairs={{0,8},{8,0},{16,24},{24,16},{1,9},{9,1},{17,25},{25,17},{2,10},{10... | collective-permute-start | bytes 1572872 | tf_op jit(solution)/shard_map/ppermute | solution.py:167
  69.4 0.8 %copy-start.5 = (bf16[4,4,32,512]{3,2,1,0:T(8,128)(2,1)}, bf16[4,4,32,512]{3,2,1,0:T(8,128)(2,1)S(1)}, u32[]{:S(2)}) copy-start(bf16[4,4,32,512]{3,2,1,0:T(8,128)(2,1)S(1)} %collective-permute-done.9.far) | copy-start | bytes 1572868

commit v2 on v1

--- a/solution.py
+++ b/solution.py
@@ -13,43 +13,65 @@
 NT = (((1,), (1,)), ((), ()))
 NN = (((1,), (0,)), ((), ()))
 VMEM = pl.BlockSpec(memory_space=pltpu.VMEM)
-SMEM = pl.BlockSpec(memory_space=pltpu.SMEM)
+HBM = pl.BlockSpec(memory_space=pltpu.HBM)
 
 
 def dot(a, b, dims):
     return lax.dot_general(a, b, dims, preferred_element_type=F32)
 
 
-def project_kernel(n_col, lengths, hidden, proj_in_t, grads, proj_out, out, grads_f32, weights):
-    dest = pl.program_id(0)
+def project_kernel(n_row, n_col, lengths, hidden, proj_in_t, grads, proj_out, out, *scratch):
+    lengths_s, hidden_s, proj_s, grads_s, weights_s, grads_f32, weights, blocks, sems, chunk_sems, out_sems = scratch
     rows, queries, tokens = grads.shape
-    q_dest, t_part, columns = hidden.shape
+    columns = hidden.shape[2]
+    t_part = hidden.shape[1]
     width = proj_out.shape[1]
-
-    @pl.when(dest == 0)
-    def _():
-        grads_f32[...] = grads[...].astype(F32).reshape(rows * queries, tokens)
-        i = lax.broadcasted_iota(jnp.int32, (width, width), 0)
-        j = lax.broadcasted_iota(jnp.int32, (width, width), 1)
-        half = width // 2
-        pick = j == jnp.where(i < half, 2 * i, 2 * (i - half) + 1)
-        weights[...] = dot(pick.astype(BF16), proj_out[...], NT).astype(BF16)
-
-    v = dot(proj_in_t[...], hidden[...].reshape(q_dest * t_part, columns), NT)
-    width_in = v.shape[0]
-    out[0, 0:width_in, :] = v.astype(BF16)
+    width_in = proj_in_t.shape[0]
+    group = n_row * n_col
+    q_dest = queries // group
     share = q_dest // n_col
+    dests = 2
+    pairs = ((proj_in_t, proj_s), (proj_out, weights_s), (grads, grads_s), (lengths, lengths_s))
+    small = [pltpu.make_async_copy(src, dst, sems.at[i]) for i, (src, dst) in enumerate(pairs)]
+    chunks = []
+    for i in range(group // dests):
+        part = pl.ds(i * dests * q_dest, dests * q_dest)
+        chunks.append(pltpu.make_async_copy(hidden.at[part], hidden_s.at[part], chunk_sems.at[i]))
+    for copy in small + chunks:
+        copy.start()
+    small[0].wait()
+    proj = proj_s[...].astype(F32).T.astype(BF16)
+    for copy in small[1:]:
+        copy.wait()
+    i = lax.broadcasted_iota(jnp.int32, (width, width), 0)
+    j = lax.broadcasted_iota(jnp.int32, (width, width), 1)
+    half = width // 2
+    pick = j == jnp.where(i < half, 2 * i, 2 * (i - half) + 1)
+    weights[...] = dot(pick.astype(BF16), weights_s[...], NT).astype(BF16)
+    grads_f32[...] = grads_s[...].astype(F32).reshape(rows * queries, tokens)
     lane = lax.broadcasted_iota(jnp.int32, (width, tokens), 1)
-    for i in range(share):
-        q = dest * q_dest + lax.axis_index("col") * share + i
-        g = grads_f32[pl.ds(q, rows, stride=queries), :].astype(BF16)
-        u = dot(weights[...], g, NN)
-        u = jnp.where(lane < lengths[q], u, 0.0)
-        at = width_in + i * width
-        out[0, at : at + width, :] = u.astype(BF16)
-
-
-def feature_kernel(n_row, n_col, q_dest, width, width_in, copies, got, out, held):
+    outs = [pltpu.make_async_copy(blocks.at[g], out.at[g], out_sems.at[g]) for g in range(group)]
+    for dest in range(group):
+        for i in range(share):
+            q = dest * q_dest + lax.axis_index("col") * share + i
+            g = grads_f32[pl.ds(q, rows, stride=queries), :].astype(BF16)
+            u = jnp.where(lane < lengths_s[q], dot(weights[...], g, NN), 0.0)
+            at = width_in + i * width
+            blocks[dest, at : at + width, :] = u.astype(BF16)
+        if dest % dests == dests - 1:
+            i = dest // dests
+            chunks[i].wait()
+            part = hidden_s[i * dests * q_dest : (i + 1) * dests * q_dest]
+            v = dot(part.reshape(dests * q_dest * t_part, columns), proj, NN)
+            for k in range(dests):
+                g = i * dests + k
+                blocks[g, 0:width_in, :] = v[k * tokens : (k + 1) * tokens].T.astype(BF16)
+                outs[g].start()
+    for copy in outs:
+        copy.wait()
+
+
+def feature_kernel(n_row, n_col, q_dest, width, width_in, copies, got, out, held, made, sem):
     tokens = got.shape[2]
     t_part = tokens // q_dest
     share = q_dest // n_col
@@ -81,7 +103,10 @@
     for r in range(n_row):
         block = held[r * n : (r + 1) * n, :].astype(BF16)
         for k in range(copies):
-            out[r * copies + k] = block
+            made[r * copies + k] = block
+    copy = pltpu.make_async_copy(made, out, sem)
+    copy.start()
+    copy.wait()
 
 
 def condition_kernel(n_row, n_col, q_dest, got, p_own, p_got, keep, send, got_f32):
@@ -120,23 +145,26 @@
     out[...] = (mine[...] + got[...]).astype(BF16)
 
 
-def score_kernel(n_row, n_col, n_store, q_dest, near, far, stored, out, held, ordered):
-    sources, width = near.shape[2:]
+def score_kernel(n_row, n_col, n_store, q_dest, iy, last, near, far, stored, *refs):
+    n_x, _, sources, width = near.shape
     row, col, store = (lax.axis_index(a) for a in AXES)
     x, core = row // 2, lax.rem(row, 2)
-    n_x = n_row // 2
     acc = None
-    for iy in range(n_col):
-        for iz in range(n_store):
-            y, z = lax.bitwise_xor(col, iy), lax.bitwise_xor(store, iz)
-            at = pl.multiple_of((z * n_col + y) * width, width)
-            left = jnp.concatenate([ref[ix * n_col + iy, iz] for ref in (near, far) for ix in range(n_x)], axis=0)
-            term = dot(left, stored[:, pl.ds(at, width)], NT)
-            acc = term if acc is None else acc + term
+    for iz in range(n_store):
+        y, z = lax.bitwise_xor(col, iy), lax.bitwise_xor(store, iz)
+        at = pl.multiple_of((z * n_col + y) * width, width)
+        left = jnp.concatenate([ref[ix, iz] for ref in (near, far) for ix in range(n_x)], axis=0)
+        term = dot(left, stored[:, pl.ds(at, width)], NT)
+        acc = term if acc is None else acc + term
+    if not last:
+        refs[0][...] = acc
+        return
+    before, out, held, ordered = refs
+    acc += before[...]
     lanes = held.shape[2]
+    group = n_row * n_col
     for i in range(held.shape[0]):
         held[i] = acc[:, i * lanes : (i + 1) * lanes]
-    group = n_row * n_col
     for i in range(held.shape[0]):
         for side in range(2):
             for ix in range(n_x):
@@ -148,13 +176,14 @@
         out[:, i * lanes : (i + 1) * lanes] = ordered[i]
 
 
-def call(kernel, outs, in_specs, scratch=(), flops=0, size=0, **more):
+def call(kernel, outs, in_specs, scratch=(), flops=0, size=0, vmem=12, **more):
     return pl.pallas_call(
         kernel,
         out_shape=outs,
         in_specs=in_specs,
         scratch_shapes=list(scratch),
         cost_estimate=pl.CostEstimate(flops=flops, bytes_accessed=size, transcendentals=0),
+        compiler_params=pltpu.CompilerParams(vmem_limit_bytes=vmem << 20),
         **more,
     )
 
@@ -182,21 +211,27 @@
     p_send = lax.dynamic_slice_in_dim(precond, (1 - col) * j_width, j_width, axis=1)
     p_got = swap(p_send, "col", n_col, 1)
 
-    const = lambda nd: (lambda i: (0,) * nd)
-    blocks = pl.pallas_call(
-        functools.partial(project_kernel, n_col),
-        grid=(group,),
-        in_specs=[
-            SMEM,
-            pl.BlockSpec((q_dest, t_part, columns), lambda i: (i, 0, 0)),
-            pl.BlockSpec((width_in, columns), const(2)),
-            pl.BlockSpec(out_grads.shape, const(3)),
-            pl.BlockSpec(proj_out.shape, const(2)),
+    blocks = call(
+        functools.partial(project_kernel, n_row, n_col),
+        shape((group, depth, tokens), BF16),
+        [HBM] * 5,
+        [
+            pltpu.SMEM(lengths.shape, jnp.int32),
+            pltpu.VMEM(hidden.shape, BF16),
+            pltpu.VMEM((width_in, columns), BF16),
+            pltpu.VMEM(out_grads.shape, BF16),
+            pltpu.VMEM(proj_out.shape, BF16),
+            pltpu.VMEM((rows * queries, tokens), F32),
+            pltpu.VMEM((width, rows), BF16),
+            pltpu.VMEM((group, depth, tokens), BF16),
+            pltpu.SemaphoreType.DMA((4,)),
+            pltpu.SemaphoreType.DMA((group // 2,)),
+            pltpu.SemaphoreType.DMA((group,)),
         ],
-        out_specs=pl.BlockSpec((1, depth, tokens), lambda i: (i, 0, 0)),
-        out_shape=shape((group, depth, tokens), BF16),
-        scratch_shapes=[pltpu.VMEM((rows * queries, tokens), F32), pltpu.VMEM((width, rows), BF16)],
-        cost_estimate=pl.CostEstimate(flops=2 * hidden.size * width_in, bytes_accessed=2 * hidden.size, transcendentals=0),
+        flops=2 * hidden.size * width_in,
+        size=2 * hidden.size,
+        out_specs=HBM,
+        vmem=60,
     )(lengths, hidden, proj_in.T, out_grads, proj_out)
     got = lax.all_to_all(blocks, ("row", "col"), 0, 0)
 
@@ -207,8 +242,9 @@
         functools.partial(feature_kernel, n_row, n_col, q_dest, width, width_in, copies),
         shape((n_row * copies, n, tokens), BF16),
         [VMEM],
-        [pltpu.VMEM((half * q_dest, tokens), F32)],
+        [pltpu.VMEM((half * q_dest, tokens), F32), pltpu.VMEM((n_row * copies, n, tokens), BF16), pltpu.SemaphoreType.DMA],
         size=2 * got.size,
+        out_specs=HBM,
     )(got)
     feats = lax.all_to_all(feats, AXES, 0, 0)
 
@@ -230,22 +266,18 @@
     cond = jnp.stack([cond] + [swap(cond, "store", n_store, k) for k in range(1, n_store)])
     pairs = lambda a, k: [(i, i ^ k) for i in range(a)]
     diag = [(r * n_col + c, (r ^ 2) * n_col + (c ^ 1)) for r in range(n_row) for c in range(n_col)]
-    near = jnp.stack(
-        [
-            cond,
-            swap(cond, "col", n_col, 1),
-            swap(cond, "row", n_row, 2),
-            lax.ppermute(cond, ("row", "col"), diag),
-        ]
-    )
+    from_x = swap(cond, "row", n_row, 2)
+    from_y = swap(cond, "col", n_col, 1)
+    from_xy = lax.ppermute(cond, ("row", "col"), diag)
+    scores = shape((sources * q_dest, stored.shape[0]), F32)
+    score = functools.partial(score_kernel, n_row, n_col, n_store, q_dest)
+    near = jnp.stack([cond, from_x])
     far = swap(near, "row", n_row, 1)
-    return call(
-        functools.partial(score_kernel, n_row, n_col, n_store, q_dest),
-        shape((sources * q_dest, stored.shape[0]), F32),
-        [VMEM, VMEM, VMEM],
-        [pltpu.VMEM((stored.shape[0] // 128, sources * q_dest, 128), F32)] * 2,
-        size=2 * stored.size,
-    )(near, far, stored)
+    part = call(functools.partial(score, 0, False), scores, [VMEM] * 3, size=stored.size)(near, far, stored)
+    near = jnp.stack([from_y, from_xy])
+    far = swap(near, "row", n_row, 1)
+    held = pltpu.VMEM((stored.shape[0] // 128, sources * q_dest, 128), F32)
+    return call(functools.partial(score, 1, True), scores, [VMEM] * 4, [held, held], size=stored.size)(near, far, stored, part)
 
 
 def plain_device(hidden, out_grads, proj_out, proj_in, lengths, precond, stored):

time: 74.8 us -> 61.6 us (0.82)
  Pallas kernels: 19.5 us -> 9.02 us
  waiting for transfers between devices: 29 us -> 26.5 us
  other arithmetic: 0.85 us -> 0.08 us
    pallas_call x2 -> x3, Pallas kernels: 11.4 us -> 6.72 us  [the longest x1 4.77 us: split_device(): call(functools.partial(project_kernel, n_row, n_col), shape((group, depth...]
    all_to_all x1, waiting for transfers between devices: 7.31 us -> 4.45 us  [split_device(): feats = lax.all_to_all(feats, AXES, 0, 0)]
    dynamic_slice x1, local copies, waits for them, and re-layouts: 0.04 us -> 1.87 us  [split_device(): lax.dynamic_slice_in_dim(precond, (1 - col) * j_width, j_width, axis=1)]
    all_to_all x1, waiting for transfers between devices: 5.28 us -> 3.52 us  [split_device(): got = lax.all_to_all(blocks, ('row', 'col'), 0, 0)]
    pallas_call x1, Pallas kernels: 2.34 us -> 0.68 us  [split_device(): call(functools.partial(feature_kernel, n_row, n_col, q_dest, width, width...]
    pallas_call x1, Pallas kernels: 1.64 us -> 0.02 us  [split_device(): call(fold_kernel, (piece, piece), [VMEM, VMEM], size=keep.size * 8)]
    unnamed x16 -> x6, local copies, waits for them, and re-layouts: 3.54 us -> 1.94 us
    ppermute x9 -> x10, waiting for transfers between devices: 14.9 us -> 16.4 us  [swap(): return lax.ppermute(x, axis, [(i, i ^ k) for i in range(n)])]
  transfers between devices with their start and end apart: 12 -> 13, of which waited for: 11 -> 11; matrix products, arithmetic and copies ran while one was open for 0% -> 3% of each run, Pallas kernels for 3% -> 2%
where the time goes in v2:
time: 61.6 us; the launch traced here: 61.2 us
  waiting for transfers between devices  26.5 us (43%)
  starting transfers between devices  21.7 us (35%)
  Pallas kernels  9.02 us (15%)
  local copies, waits for them, and re-layouts  3.81 us (6%)
    ppermute x10, waiting for transfers between devices, swap(): return lax.ppermute(x, axis, [(i, i ^ k) for i in range(n)])  16.4 us
    ppermute x10, starting transfers between devices, swap(): return lax.ppermute(x, axis, [(i, i ^ k) for i in range(n)])  10 us
    all_to_all x1, starting transfers between devices, split_device(): got = lax.all_to_all(blocks, ('row', 'col'), 0, 0)  5.48 us
    all_to_all x1, starting transfers between devices, split_device(): feats = lax.all_to_all(feats, AXES, 0, 0)  4.86 us
    pallas_call x1, Pallas kernels, split_device(): call(functools.partial(project_kernel, n_row, n_col), shape((group, depth...  4.77 us
    all_to_all x1, waiting for transfers between devices, split_device(): feats = lax.all_to_all(feats, AXES, 0, 0)  4.45 us
    all_to_all x1, waiting for transfers between devices, split_device(): got = lax.all_to_all(blocks, ('row', 'col'), 0, 0)  3.52 us
    ppermute x1, waiting for transfers between devices, split_device(): from_xy = lax.ppermute(cond, ('row', 'col'), diag)  2.13 us
  transfers between devices with their start and end apart: 13, of which 11 were waited for; matrix products, arithmetic and copies ran while one was open for 3% of the time, Pallas kernels for 2%

profile of v2, /device:TPU:0, one launch (start us, length us, event | category | flops | bytes accessed | tf_op | source)
XLA Modules:
  0.0 61.2 jit_solution(3057843002399308436)
XLA Ops:
  0.0 4.8 %shard_map.73 = bf16[8,192,128]{2,1,0:T(8,128)(2,1)} custom-call(s32[32]{0:T(128)} %lengths.1, bf16[32,32,2048]{2,1,0:T(8,128)(2,1)} %hidden.1, bf16[64,2048]{1,0:T(8,128)(2,1)} %bitcast.11, bf16[52,32,128]{2,1,0:T(8,128)(2,1)} %grads.1, bf16[52,64]{1,0:T(8,128)(2,1)} %proj_out.1), custom_call_target="tpu_custom_call" | custom-call | flops 268435456 | bytes 4194304 | tf_op jit(solution)/shard_map/pallas_call | solution.py:214
  4.8 5.5 %all-to-all-start = ((bf16[8,192,128]{2,1,0:T(8,128)(2,1)}), bf16[8,192,128]{2,1,0:T(8,128)(2,1)S(1)}, u32[]{:S(2)}, u32[]{:S(2)}) async-start(bf16[8,192,128]{2,1,0:T(8,128)(2,1)} %shard_map.73), calls=%async_computation | async-start | bytes 786432 | tf_op jit(solution)/shard_map/all_to_all | solution.py:236
  10.3 1.9 %constant_dynamic-slice_fusion = bf16[512,512]{1,0:T(8,128)(2,1)} fusion(bf16[512,1024]{1,0:T(8,128)(2,1)} %p_own.1, s32[]{:T(128)S(6)} %select_n.3), kind=kLoop, calls=%fused_computation.3 | loop fusion | bytes 1048580 | tf_op jit(solution)/shard_map/dynamic_slice | solution.py:211
  12.1 2.0 %collective-permute-start = (bf16[512,512]{1,0:T(8,128)(2,1)}, bf16[512,512]{1,0:T(8,128)(2,1)}, u32[]{:S(2)}, u32[]{:S(2)}) collective-permute-start(bf16[512,512]{1,0:T(8,128)(2,1)} %constant_dynamic-slice_fusion), channel_id=1, source_target_pairs={{0,4},{4,0},{1,5},{5,1},{2,6},{6,2},{3,7},{7,3},{8,12},{12,8},{9,1... | collective-permute-start | bytes 1572872 | tf_op jit(solution)/shard_map/ppermute | solution.py:196
  14.2 3.5 %all-to-all-done.got = bf16[8,192,128]{2,1,0:T(8,128)(2,1)S(1)} async-done(((bf16[8,192,128]{2,1,0:T(8,128)(2,1)}), bf16[8,192,128]{2,1,0:T(8,128)(2,1)S(1)}, u32[]{:S(2)}, u32[]{:S(2)}) %all-to-all-start) | async-done | bytes 393248 | tf_op jit(solution)/shard_map/all_to_all | solution.py:236
  19.1 4.9 %all-to-all-start.1 = ((bf16[32,32,128]{2,1,0:T(8,128)(2,1)}), bf16[32,32,128]{2,1,0:T(8,128)(2,1)S(1)}, u32[]{:S(2)}, u32[]{:S(2)}) async-start(bf16[32,32,128]{2,1,0:T(8,128)(2,1)} %copy-done.2), calls=%async_computation.1 | async-start | bytes 524288 | tf_op jit(solution)/shard_map/all_to_all | solution.py:249
  24.0 6.3 %collective-permute-done.p_got = bf16[512,512]{1,0:T(8,128)(2,1)} collective-permute-done((bf16[512,512]{1,0:T(8,128)(2,1)}, bf16[512,512]{1,0:T(8,128)(2,1)}, u32[]{:S(2)}, u32[]{:S(2)}) %collective-permute-start) | collective-permute-done | bytes 524320 | tf_op jit(solution)/shard_map/ppermute | solution.py:196
  30.2 4.5 %all-to-all-done.1.got = bf16[32,32,128]{2,1,0:T(8,128)(2,1)S(1)} async-done(((bf16[32,32,128]{2,1,0:T(8,128)(2,1)}), bf16[32,32,128]{2,1,0:T(8,128)(2,1)S(1)}, u32[]{:S(2)}, u32[]{:S(2)}) %all-to-all-start.1) | async-done | bytes 262176 | tf_op jit(solution)/shard_map/all_to_all | solution.py:249
  34.7 1.2 %copy-done.1 = bf16[512,1024]{1,0:T(8,128)(2,1)S(1)} copy-done((bf16[512,1024]{1,0:T(8,128)(2,1)S(1)}, bf16[512,1024]{1,0:T(8,128)(2,1)}, u32[]{:S(2)}) %copy-start.1) | copy-done | bytes 1048600
  35.9 1.6 %shard_map.75 = (f32[2,32,512]{2,1,0:T(8,128)S(1)}, f32[2,32,512]{2,1,0:T(8,128)S(1)}) custom-call(bf16[32,32,128]{2,1,0:T(8,128)(2,1)S(1)} %all-to-all-done.1.got, bf16[512,1024]{1,0:T(8,128)(2,1)S(1)} %copy-done.1, bf16[512,512]{1,0:T(8,128)(2,1)} %collective-permute-done.p_got), custom_call_target="tpu_custom_call" | custom-call | bytes 1048576 | tf_op jit(solution)/shard_map/pallas_call | solution.py:253
  37.7 1.2 %collective-permute-done.1.got = f32[2,32,512]{2,1,0:T(8,128)S(1)} collective-permute-done((f32[2,32,512]{2,1,0:T(8,128)S(1)}, f32[2,32,512]{2,1,0:T(8,128)S(1)}, u32[]{:S(2)}, u32[]{:S(2)}) %collective-permute-start.1) | collective-permute-done | bytes 131104 | tf_op jit(solution)/shard_map/ppermute | solution.py:196
  39.0 1.0 %collective-permute-start.2 = (f32[32,512]{1,0:T(8,128)S(1)}, f32[32,512]{1,0:T(8,128)S(1)}, u32[]{:S(2)}, u32[]{:S(2)}) collective-permute-start(f32[32,512]{1,0:T(8,128)S(1)} %get-tuple-element.12), channel_id=1, source_target_pairs={{0,16},{8,24},{16,0},{24,8},{1,17},{9,25},{17,1},{25,9},{2,18},{10... | collective-permute-start | bytes 196616 | tf_op jit(solution)/shard_map/ppermute | solution.py:196
  39.9 3.4 %collective-permute-done.2.got = f32[32,512]{1,0:T(8,128)S(1)} collective-permute-done((f32[32,512]{1,0:T(8,128)S(1)}, f32[32,512]{1,0:T(8,128)S(1)}, u32[]{:S(2)}, u32[]{:S(2)}) %collective-permute-start.2) | collective-permute-done | bytes 65568 | tf_op jit(solution)/shard_map/ppermute | solution.py:196
  44.0 1.0 %collective-permute-start.4 = (bf16[32,512]{1,0:T(8,128)(2,1)S(1)}, bf16[32,512]{1,0:T(8,128)(2,1)S(1)}, u32[]{:S(2)}, u32[]{:S(2)}) collective-permute-start(bf16[32,512]{1,0:T(8,128)(2,1)S(1)} %shard_map.77), channel_id=1, source_target_pairs={{0,2},{1,3},{2,0},{3,1},{4,6},{5,7},{6,4},{7,5},{8,10},{9,11},{10,... | collective-permute-start | bytes 98312 | tf_op jit(solution)/shard_map/ppermute | solution.py:196
  45.0 2.7 %collective-permute-start.3 = (bf16[32,512]{1,0:T(8,128)(2,1)S(1)}, bf16[32,512]{1,0:T(8,128)(2,1)S(1)}, u32[]{:S(2)}, u32[]{:S(2)}) collective-permute-start(bf16[32,512]{1,0:T(8,128)(2,1)S(1)} %shard_map.77), channel_id=1, source_target_pairs={{0,1},{1,0},{2,3},{3,2},{4,5},{5,4},{6,7},{7,6},{8,9},{9,8},{10,11... | collective-permute-start | bytes 98312 | tf_op jit(solution)/shard_map/ppermute | solution.py:196
  47.7 1.4 %collective-permute-done.5 = bf16[32,512]{1,0:T(8,128)(2,1)S(1)} collective-permute-done((bf16[32,512]{1,0:T(8,128)(2,1)S(1)}, bf16[32,512]{1,0:T(8,128)(2,1)S(1)}, u32[]{:S(2)}, u32[]{:S(2)}) %collective-permute-start.5) | collective-permute-done | bytes 32800 | tf_op jit(solution)/shard_map/ppermute | solution.py:196
  49.7 1.3 %collective-permute-start.9 = (bf16[4,32,512]{2,1,0:T(8,128)(2,1)S(1)}, bf16[4,32,512]{2,1,0:T(8,128)(2,1)S(1)}, u32[]{:S(2)}, u32[]{:S(2)}) collective-permute-start(bf16[4,32,512]{2,1,0:T(8,128)(2,1)S(1)} %get-tuple-element.14), channel_id=1, source_target_pairs={{0,16},{8,24},{16,0},{24,8},{1,17},{9,25},{17,1},{25,9},{2,18},{10... | collective-permute-start | bytes 393224 | tf_op jit(solution)/shard_map/ppermute | solution.py:196
  51.0 1.3 %collective-permute-start.7 = (bf16[4,32,512]{2,1,0:T(8,128)(2,1)S(1)}, bf16[4,32,512]{2,1,0:T(8,128)(2,1)S(1)}, u32[]{:S(2)}, u32[]{:S(2)}) collective-permute-start(bf16[4,32,512]{2,1,0:T(8,128)(2,1)S(1)} %get-tuple-element.14), channel_id=1, source_target_pairs={{0,20},{4,16},{8,28},{12,24},{16,4},{20,0},{24,12},{28,8},{1,21},{... | collective-permute-start | bytes 393224 | tf_op jit(solution)/shard_map/ppermute | solution.py:271
  52.2 1.0 %collective-permute-start.6 = (bf16[4,32,512]{2,1,0:T(8,128)(2,1)S(1)}, bf16[4,32,512]{2,1,0:T(8,128)(2,1)S(1)}, u32[]{:S(2)}, u32[]{:S(2)}) collective-permute-start(bf16[4,32,512]{2,1,0:T(8,128)(2,1)S(1)} %get-tuple-element.14), channel_id=1, source_target_pairs={{0,4},{4,0},{1,5},{5,1},{2,6},{6,2},{3,7},{7,3},{8,12},{12,8},{9,1... | collective-permute-start | bytes 393224 | tf_op jit(solution)/shard_map/ppermute | solution.py:196
  53.2 1.5 %collective-permute-done.9 = bf16[4,32,512]{2,1,0:T(8,128)(2,1)S(1)} collective-permute-done((bf16[4,32,512]{2,1,0:T(8,128)(2,1)S(1)}, bf16[4,32,512]{2,1,0:T(8,128)(2,1)S(1)}, u32[]{:S(2)}, u32[]{:S(2)}) %collective-permute-start.9) | collective-permute-done | bytes 131104 | tf_op jit(solution)/shard_map/ppermute | solution.py:196
  54.8 2.1 %collective-permute-done.7 = bf16[4,32,512]{2,1,0:T(8,128)(2,1)S(1)} collective-permute-done((bf16[4,32,512]{2,1,0:T(8,128)(2,1)S(1)}, bf16[4,32,512]{2,1,0:T(8,128)(2,1)S(1)}, u32[]{:S(2)}, u32[]{:S(2)}) %collective-permute-start.7) | collective-permute-done | bytes 131104 | tf_op jit(solution)/shard_map/ppermute | solution.py:271
  56.9 1.3 %collective-permute-done.6 = bf16[4,32,512]{2,1,0:T(8,128)(2,1)S(1)} collective-permute-done((bf16[4,32,512]{2,1,0:T(8,128)(2,1)S(1)}, bf16[4,32,512]{2,1,0:T(8,128)(2,1)S(1)}, u32[]{:S(2)}, u32[]{:S(2)}) %collective-permute-start.6) | collective-permute-done | bytes 131104 | tf_op jit(solution)/shard_map/ppermute | solution.py:196
  59.0 0.9 %collective-permute-done.8.far = bf16[2,4,32,512]{3,2,1,0:T(8,128)(2,1)S(1)} collective-permute-done((bf16[2,4,32,512]{3,2,1,0:T(8,128)(2,1)S(1)}, bf16[2,4,32,512]{3,2,1,0:T(8,128)(2,1)S(1)}, u32[]{:S(2)}, u32[]{:S(2)}) %collective-permute-start.8) | collective-permute-done | bytes 262176 | tf_op jit(solution)/shard_map/ppermute | solution.py:196
  59.9 1.3 %shard_map.79 = f32[128,384]{1,0:T(8,128)} custom-call(bf16[2,4,32,512]{3,2,1,0:T(8,128)(2,1)S(1)} %pad_maximum_fusion.near, bf16[2,4,32,512]{3,2,1,0:T(8,128)(2,1)S(1)} %collective-permute-done.8.far, bf16[384,4096]{1,0:T(8,128)(2,1)S(1)} %copy-done, f32[128,384]{1,0:T(8,128)S(1)} %shard_map.78.refs_0_), custom_call_target="tpu_custom_call" | custom-call | bytes 1572864 | tf_op jit(solution)/shard_map/pallas_call | solution.py:280
  (19 shorter events, 3.6 us)
Async XLA Ops:
  4.8 53.6 %copy-start = (bf16[384,4096]{1,0:T(8,128)(2,1)S(1)}, bf16[384,4096]{1,0:T(8,128)(2,1)}, u32[]{:S(2)}) copy-start(bf16[384,4096]{1,0:T(8,128)(2,1)} %stored.3) | copy-start | bytes 9437188
  4.8 12.9 %all-to-all-start = ((bf16[8,192,128]{2,1,0:T(8,128)(2,1)}), bf16[8,192,128]{2,1,0:T(8,128)(2,1)S(1)}, u32[]{:S(2)}, u32[]{:S(2)}) async-start(bf16[8,192,128]{2,1,0:T(8,128)(2,1)} %shard_map.73), calls=%async_computation | async-start | bytes 786432 | tf_op jit(solution)/shard_map/all_to_all | solution.py:236
  12.1 18.1 %collective-permute-start = (bf16[512,512]{1,0:T(8,128)(2,1)}, bf16[512,512]{1,0:T(8,128)(2,1)}, u32[]{:S(2)}, u32[]{:S(2)}) collective-permute-start(bf16[512,512]{1,0:T(8,128)(2,1)} %constant_dynamic-slice_fusion), channel_id=1, source_target_pairs={{0,4},{4,0},{1,5},{5,1},{2,6},{6,2},{3,7},{7,3},{8,12},{12,8},{9,1... | collective-permute-start | bytes 1572872 | tf_op jit(solution)/shard_map/ppermute | solution.py:196
  18.4 0.7 %copy-start.2 = (bf16[32,32,128]{2,1,0:T(8,128)(2,1)}, bf16[32,32,128]{2,1,0:T(8,128)(2,1)S(1)}, u32[]{:S(2)}) copy-start(bf16[32,32,128]{2,1,0:T(8,128)(2,1)S(1)} %shard_map.74) | copy-start | bytes 786436
  19.1 15.6 %all-to-all-start.1 = ((bf16[32,32,128]{2,1,0:T(8,128)(2,1)}), bf16[32,32,128]{2,1,0:T(8,128)(2,1)S(1)}, u32[]{:S(2)}, u32[]{:S(2)}) async-start(bf16[32,32,128]{2,1,0:T(8,128)(2,1)} %copy-done.2), calls=%async_computation.1 | async-start | bytes 524288 | tf_op jit(solution)/shard_map/all_to_all | solution.py:249
  34.7 1.2 %copy-start.1 = (bf16[512,1024]{1,0:T(8,128)(2,1)S(1)}, bf16[512,1024]{1,0:T(8,128)(2,1)}, u32[]{:S(2)}) copy-start(bf16[512,1024]{1,0:T(8,128)(2,1)} %p_own.1) | copy-start | bytes 3145732
  37.5 1.4 %collective-permute-start.1 = (f32[2,32,512]{2,1,0:T(8,128)S(1)}, f32[2,32,512]{2,1,0:T(8,128)S(1)}, u32[]{:S(2)}, u32[]{:S(2)}) collective-permute-start(f32[2,32,512]{2,1,0:T(8,128)S(1)} %get-tuple-element.10), channel_id=1, source_target_pairs={{0,8},{8,0},{16,24},{24,16},{1,9},{9,1},{17,25},{25,17},{2,10},{10... | collective-permute-start | bytes 393224 | tf_op jit(solution)/shard_map/ppermute | solution.py:196
  39.0 4.3 %collective-permute-start.2 = (f32[32,512]{1,0:T(8,128)S(1)}, f32[32,512]{1,0:T(8,128)S(1)}, u32[]{:S(2)}, u32[]{:S(2)}) collective-permute-start(f32[32,512]{1,0:T(8,128)S(1)} %get-tuple-element.12), channel_id=1, source_target_pairs={{0,16},{8,24},{16,0},{24,8},{1,17},{9,25},{17,1},{25,9},{2,18},{10... | collective-permute-start | bytes 196616 | tf_op jit(solution)/shard_map/ppermute | solution.py:196
  43.3 5.8 %collective-permute-start.5 = (bf16[32,512]{1,0:T(8,128)(2,1)S(1)}, bf16[32,512]{1,0:T(8,128)(2,1)S(1)}, u32[]{:S(2)}, u32[]{:S(2)}) collective-permute-start(bf16[32,512]{1,0:T(8,128)(2,1)S(1)} %shard_map.77), channel_id=1, source_target_pairs={{0,3},{1,2},{2,1},{3,0},{4,7},{5,6},{6,5},{7,4},{8,11},{9,10},{10,... | collective-permute-start | bytes 98312 | tf_op jit(solution)/shard_map/ppermute | solution.py:196
  44.0 5.2 %collective-permute-start.4 = (bf16[32,512]{1,0:T(8,128)(2,1)S(1)}, bf16[32,512]{1,0:T(8,128)(2,1)S(1)}, u32[]{:S(2)}, u32[]{:S(2)}) collective-permute-start(bf16[32,512]{1,0:T(8,128)(2,1)S(1)} %shard_map.77), channel_id=1, source_target_pairs={{0,2},{1,3},{2,0},{3,1},{4,6},{5,7},{6,4},{7,5},{8,10},{9,11},{10,... | collective-permute-start | bytes 98312 | tf_op jit(solution)/shard_map/ppermute | solution.py:196
  45.0 4.6 %collective-permute-start.3 = (bf16[32,512]{1,0:T(8,128)(2,1)S(1)}, bf16[32,512]{1,0:T(8,128)(2,1)S(1)}, u32[]{:S(2)}, u32[]{:S(2)}) collective-permute-start(bf16[32,512]{1,0:T(8,128)(2,1)S(1)} %shard_map.77), channel_id=1, source_target_pairs={{0,1},{1,0},{2,3},{3,2},{4,5},{5,4},{6,7},{7,6},{8,9},{9,8},{10,11... | collective-permute-start | bytes 98312 | tf_op jit(solution)/shard_map/ppermute | solution.py:196
  49.7 5.0 %collective-permute-start.9 = (bf16[4,32,512]{2,1,0:T(8,128)(2,1)S(1)}, bf16[4,32,512]{2,1,0:T(8,128)(2,1)S(1)}, u32[]{:S(2)}, u32[]{:S(2)}) collective-permute-start(bf16[4,32,512]{2,1,0:T(8,128)(2,1)S(1)} %get-tuple-element.14), channel_id=1, source_target_pairs={{0,16},{8,24},{16,0},{24,8},{1,17},{9,25},{17,1},{25,9},{2,18},{10... | collective-permute-start | bytes 393224 | tf_op jit(solution)/shard_map/ppermute | solution.py:196
  51.0 6.0 %collective-permute-start.7 = (bf16[4,32,512]{2,1,0:T(8,128)(2,1)S(1)}, bf16[4,32,512]{2,1,0:T(8,128)(2,1)S(1)}, u32[]{:S(2)}, u32[]{:S(2)}) collective-permute-start(bf16[4,32,512]{2,1,0:T(8,128)(2,1)S(1)} %get-tuple-element.14), channel_id=1, source_target_pairs={{0,20},{4,16},{8,28},{12,24},{16,4},{20,0},{24,12},{28,8},{1,21},{... | collective-permute-start | bytes 393224 | tf_op jit(solution)/shard_map/ppermute | solution.py:271
  52.2 6.0 %collective-permute-start.6 = (bf16[4,32,512]{2,1,0:T(8,128)(2,1)S(1)}, bf16[4,32,512]{2,1,0:T(8,128)(2,1)S(1)}, u32[]{:S(2)}, u32[]{:S(2)}) collective-permute-start(bf16[4,32,512]{2,1,0:T(8,128)(2,1)S(1)} %get-tuple-element.14), channel_id=1, source_target_pairs={{0,4},{4,0},{1,5},{5,1},{2,6},{6,2},{3,7},{7,3},{8,12},{12,8},{9,1... | collective-permute-start | bytes 393224 | tf_op jit(solution)/shard_map/ppermute | solution.py:196
  54.7 3.6 %collective-permute-start.10 = (bf16[2,4,32,512]{3,2,1,0:T(8,128)(2,1)S(1)}, bf16[2,4,32,512]{3,2,1,0:T(8,128)(2,1)S(1)}, u32[]{:S(2)}, u32[]{:S(2)}) collective-permute-start(bf16[2,4,32,512]{3,2,1,0:T(8,128)(2,1)S(1)} %pad_maximum_fusion.1.near), channel_id=1, source_target_pairs={{0,8},{8,0},{16,24},{24,16},{1,9},{9,1},{17,25},{25,17},{2,10},{10... | collective-permute-start | bytes 786440 | tf_op jit(solution)/shard_map/ppermute | solution.py:196
  58.3 1.6 %collective-permute-start.8 = (bf16[2,4,32,512]{3,2,1,0:T(8,128)(2,1)S(1)}, bf16[2,4,32,512]{3,2,1,0:T(8,128)(2,1)S(1)}, u32[]{:S(2)}, u32[]{:S(2)}) collective-permute-start(bf16[2,4,32,512]{3,2,1,0:T(8,128)(2,1)S(1)} %pad_maximum_fusion.near), channel_id=1, source_target_pairs={{0,8},{8,0},{16,24},{24,16},{1,9},{9,1},{17,25},{25,17},{2,10},{10... | collective-permute-start | bytes 786440 | tf_op jit(solution)/shard_map/ppermute | solution.py:196

commit v3 on v2

--- a/solution.py
+++ b/solution.py
@@ -37,6 +37,7 @@
     for i in range(group // dests):
         part = pl.ds(i * dests * q_dest, dests * q_dest)
         chunks.append(pltpu.make_async_copy(hidden.at[part], hidden_s.at[part], chunk_sems.at[i]))
+    col = lax.axis_index("col")
     for copy in small + chunks:
         copy.start()
     small[0].wait()
@@ -53,7 +54,7 @@
     outs = [pltpu.make_async_copy(blocks.at[g], out.at[g], out_sems.at[g]) for g in range(group)]
     for dest in range(group):
         for i in range(share):
-            q = dest * q_dest + lax.axis_index("col") * share + i
+            q = dest * q_dest + col * share + i
             g = grads_f32[pl.ds(q, rows, stride=queries), :].astype(BF16)
             u = jnp.where(lane < lengths_s[q], dot(weights[...], g, NN), 0.0)
             at = width_in + i * width
@@ -71,7 +72,9 @@
         copy.wait()
 
 
-def feature_kernel(n_row, n_col, q_dest, width, width_in, copies, got, out, held, made, sem):
+def feature_kernel(n_row, n_col, q_dest, width, width_in, copies, got, precond, out, near, held, made, sem):
+    fetch = pltpu.make_async_copy(precond, near, sem.at[1])
+    fetch.start()
     tokens = got.shape[2]
     t_part = tokens // q_dest
     share = q_dest // n_col
@@ -99,50 +102,50 @@
         total = total + pltpu.roll(total, width_in, 1)
         packed = jnp.where(lane_f < width_in, total[:half], total[half:]) * scale
         held[pl.ds(q, half, stride=q_dest), :] = packed
-    n = held.shape[0] // n_row
-    for r in range(n_row):
+    group = n_row * n_col
+    n = held.shape[0] // group
+    for r in range(group):
         block = held[r * n : (r + 1) * n, :].astype(BF16)
         for k in range(copies):
             made[r * copies + k] = block
-    copy = pltpu.make_async_copy(made, out, sem)
+    copy = pltpu.make_async_copy(made, out, sem.at[0])
     copy.start()
     copy.wait()
-
-
-def condition_kernel(n_row, n_col, q_dest, got, p_own, p_got, keep, send, got_f32):
+    fetch.wait()
+
+
+def condition_kernel(n_row, n_col, n_store, q_dest, got, precond, keep, send, got_f32):
     sources, rows, lanes = got.shape
     got_f32[...] = got[...].astype(F32).reshape(sources * rows, lanes)
-    col = lax.axis_index("col")
     core = lax.rem(lax.axis_index("row"), 2)
-    pairs = rows // q_dest
-    here = pairs // n_col
-    depth, width = p_got.shape
-    mine = pl.ds(pl.multiple_of(col * width, width), width)
-
-    def features(side, half):
+    group = n_row * n_col
+    width = keep.shape[3]
+    for ref, side in ((send, 1 - core), (keep, core)):
         columns = []
-        for i in range(here):
+        for i in range(rows // q_dest):
             blocks = []
-            for h in range(q_dest // 2):
-                at = (half * here + i) * q_dest + 2 * h + side
-                blocks.append(got_f32[pl.ds(at, sources, stride=rows), :])
+            for h in range(n_row // 2):
+                for s in range(n_store):
+                    at = s * rows + i * q_dest + 2 * h + side
+                    blocks.append(got_f32[pl.ds(at, group, stride=n_store * rows), :])
             columns.append(jnp.concatenate(blocks, axis=0).astype(BF16))
-        return jnp.concatenate(columns, axis=1)
-
-    for ref, side in ((send, 1 - core), (keep, core)):
-        acc = dot(features(side, col), p_own[:, mine], NN)
-        acc += dot(features(side, 1 - col), p_got[...], NN)
-        ref[...] = acc.reshape(ref.shape)
-
-
-def fold_kernel(keep, got, mine, other):
-    x = lax.axis_index("row") // 2
-    other[...] = keep[1 - x] + got[1 - x]
-    mine[...] = keep[x] + got[x]
-
-
-def finish_kernel(mine, got, out):
-    out[...] = (mine[...] + got[...]).astype(BF16)
+        acc = dot(jnp.concatenate(columns, axis=1), precond[...], NN)
+        for h in range(n_row // 2):
+            for y in range(n_col):
+                ref[h, y] = acc[h * sources : (h + 1) * sources, y * width : (y + 1) * width]
+
+
+def fold_kernel(keep, got, *refs):
+    x, y = lax.axis_index("row") // 2, lax.axis_index("col")
+    for ref, (a, b) in zip(refs, ((x, y), (1 - x, y), (x, 1 - y), (1 - x, 1 - y))):
+        ref[...] = keep[a, b] + got[a, b]
+
+
+def finish_kernel(*refs):
+    total = refs[0][...]
+    for ref in refs[1:-1]:
+        total += ref[...]
+    refs[-1][...] = total.astype(BF16)
 
 
 def score_kernel(n_row, n_col, n_store, q_dest, iy, last, near, far, stored, *refs):
@@ -159,20 +162,16 @@
     if not last:
         refs[0][...] = acc
         return
-    before, out, held, ordered = refs
+    before, out, ordered = refs
     acc += before[...]
-    lanes = held.shape[2]
-    group = n_row * n_col
-    for i in range(held.shape[0]):
-        held[i] = acc[:, i * lanes : (i + 1) * lanes]
-    for i in range(held.shape[0]):
+    lanes = ordered.shape[2]
+    for i in range(ordered.shape[0]):
         for side in range(2):
             for ix in range(n_x):
                 q4 = lax.bitwise_xor(x, ix) * 2 + lax.bitwise_xor(core, side)
                 base = (side * n_x + ix) * sources
-                for s in range(n_store):
-                    rows = held[i, pl.ds(base + s, group, stride=n_store), :]
-                    ordered[i, pl.ds(s * group * q_dest + q4, group, stride=q_dest), :] = rows
+                block = acc[base : base + sources, i * lanes : (i + 1) * lanes]
+                ordered[i, pl.ds(q4, sources, stride=q_dest), :] = block
         out[:, i * lanes : (i + 1) * lanes] = ordered[i]
 
 
@@ -208,12 +207,10 @@
     col = lax.axis_index("col")
     j_width = precond.shape[1] // n_col
 
-    p_send = lax.dynamic_slice_in_dim(precond, (1 - col) * j_width, j_width, axis=1)
-    p_got = swap(p_send, "col", n_col, 1)
-
+    inputs = (lengths, hidden, proj_in.T, out_grads, proj_out)
     blocks = call(
         functools.partial(project_kernel, n_row, n_col),
-        shape((group, depth, tokens), BF16),
+        pltpu.HBM((group, depth, tokens), BF16),
         [HBM] * 5,
         [
             pltpu.SMEM(lengths.shape, jnp.int32),
@@ -231,41 +228,42 @@
         flops=2 * hidden.size * width_in,
         size=2 * hidden.size,
         out_specs=HBM,
-        vmem=60,
-    )(lengths, hidden, proj_in.T, out_grads, proj_out)
+    )(*(pltpu.with_memory_space_constraint(a, pltpu.HBM) for a in inputs))
     got = lax.all_to_all(blocks, ("row", "col"), 0, 0)
 
-    copies = n_col * n_store
     half = width // 2
-    n = half * q_dest // n_row
-    feats = call(
-        functools.partial(feature_kernel, n_row, n_col, q_dest, width, width_in, copies),
-        shape((n_row * copies, n, tokens), BF16),
-        [VMEM],
-        [pltpu.VMEM((half * q_dest, tokens), F32), pltpu.VMEM((n_row * copies, n, tokens), BF16), pltpu.SemaphoreType.DMA],
+    n = half * q_dest // group
+    feats, precond = call(
+        functools.partial(feature_kernel, n_row, n_col, q_dest, width, width_in, n_store),
+        (pltpu.HBM((group * n_store, n, tokens), BF16), shape(precond.shape, BF16)),
+        [VMEM, HBM],
+        [
+            pltpu.VMEM((half * q_dest, tokens), F32),
+            pltpu.VMEM((group * n_store, n, tokens), BF16),
+            pltpu.SemaphoreType.DMA((2,)),
+        ],
         size=2 * got.size,
-        out_specs=HBM,
-    )(got)
+        out_specs=(HBM, VMEM),
+    )(got, pltpu.with_memory_space_constraint(precond, pltpu.HBM))
     feats = lax.all_to_all(feats, AXES, 0, 0)
 
     sources = group * n_store
-    part = shape((q_dest // 2, sources, j_width), F32)
+    part = shape((n_row // 2, n_col, sources, j_width), F32)
     keep, send = call(
-        functools.partial(condition_kernel, n_row, n_col, q_dest),
+        functools.partial(condition_kernel, n_row, n_col, n_store, q_dest),
         (part, part),
-        [VMEM, VMEM, VMEM],
+        [VMEM, VMEM],
         [pltpu.VMEM((sources * n, tokens), F32)],
         size=2 * precond.size,
-    )(feats, precond, p_got)
+    )(feats, precond)
     got = swap(send, "row", n_row, 1)
+    diag = [(r * n_col + c, (r ^ 2) * n_col + (c ^ 1)) for r in range(n_row) for c in range(n_col)]
     piece = shape((sources, j_width), F32)
-    mine, other = call(fold_kernel, (piece, piece), [VMEM, VMEM], size=keep.size * 8)(keep, got)
-    got = swap(other, "row", n_row, 2)
-    cond = call(finish_kernel, shape(piece.shape, BF16), [VMEM, VMEM], size=mine.size * 8)(mine, got)
+    mine, to_x, to_y, to_xy = call(fold_kernel, (piece,) * 4, [VMEM] * 2, size=keep.size * 8)(keep, got)
+    terms = (mine, swap(to_x, "row", n_row, 2), swap(to_y, "col", n_col, 1), lax.ppermute(to_xy, ("row", "col"), diag))
+    cond = call(finish_kernel, shape(piece.shape, BF16), [VMEM] * 4, size=mine.size * 8)(*terms)
 
     cond = jnp.stack([cond] + [swap(cond, "store", n_store, k) for k in range(1, n_store)])
-    pairs = lambda a, k: [(i, i ^ k) for i in range(a)]
-    diag = [(r * n_col + c, (r ^ 2) * n_col + (c ^ 1)) for r in range(n_row) for c in range(n_col)]
     from_x = swap(cond, "row", n_row, 2)
     from_y = swap(cond, "col", n_col, 1)
     from_xy = lax.ppermute(cond, ("row", "col"), diag)
@@ -277,7 +275,7 @@
     near = jnp.stack([from_y, from_xy])
     far = swap(near, "row", n_row, 1)
     held = pltpu.VMEM((stored.shape[0] // 128, sources * q_dest, 128), F32)
-    return call(functools.partial(score, 1, True), scores, [VMEM] * 4, [held, held], size=stored.size)(near, far, stored, part)
+    return call(functools.partial(score, 1, True), scores, [VMEM] * 4, [held], size=stored.size)(near, far, stored, part)
 
 
 def plain_device(hidden, out_grads, proj_out, proj_in, lengths, precond, stored):

time: 61.6 us -> 59.6 us (0.968)
  blocking collectives: 0 us -> 25.6 us
  waiting for transfers between devices: 26.5 us -> 13.2 us
  starting transfers between devices: 21.7 us -> 11.9 us
  local copies, waits for them, and re-layouts: 3.81 us -> 0.01 us
    all_to_all x0 -> x2, blocking collectives: none -> 25.6 us  [the longest x1 13.3 us: split_device(): got = lax.all_to_all(blocks, ('row', 'col'), 0, 0)]
    all_to_all x2 -> x0, starting transfers between devices: 10.3 us -> none  [the longest x1 5.48 us: split_device(): got = lax.all_to_all(blocks, ('row', 'col'), 0, 0)]
    all_to_all x2 -> x0, waiting for transfers between devices: 7.97 us -> none  [the longest x1 4.45 us: split_device(): feats = lax.all_to_all(feats, AXES, 0, 0)]
    ppermute x10, waiting for transfers between devices: 16.4 us -> 9.66 us  [swap(): return lax.ppermute(x, axis, [(i, i ^ k) for i in range(n)])]
    unnamed x6 -> x2, local copies, waits for them, and re-layouts: 1.94 us -> 0.01 us
    dynamic_slice x1 -> x0, local copies, waits for them, and re-layouts: 1.87 us -> none  [split_device(): lax.dynamic_slice_in_dim(precond, (1 - col) * j_width, j_width, axis=1)]
    ppermute x0 -> x1, starting transfers between devices: none -> 1.67 us  [split_device(): lax.ppermute(to_xy, ('row', 'col'), diag)]
    ppermute x0 -> x1, waiting for transfers between devices: none -> 1.14 us  [split_device(): lax.ppermute(to_xy, ('row', 'col'), diag)]
  transfers between devices with their start and end apart: 13 -> 12, of which waited for: 11 -> 11; matrix products, arithmetic and copies ran while one was open for 3% -> 0% of each run, Pallas kernels for 2% -> 1%
where the time goes in v3:
time: 59.6 us; the launch traced here: 59.4 us
  blocking collectives  25.6 us (43%)
  waiting for transfers between devices  13.2 us (22%)
  starting transfers between devices  11.9 us (20%)
  Pallas kernels  8.64 us (14%)
    all_to_all x1, blocking collectives, split_device(): got = lax.all_to_all(blocks, ('row', 'col'), 0, 0)  13.3 us
    all_to_all x1, blocking collectives, split_device(): feats = lax.all_to_all(feats, AXES, 0, 0)  12.3 us
    ppermute x10, waiting for transfers between devices, swap(): return lax.ppermute(x, axis, [(i, i ^ k) for i in range(n)])  9.66 us
    ppermute x10, starting transfers between devices, swap(): return lax.ppermute(x, axis, [(i, i ^ k) for i in range(n)])  9.05 us
    pallas_call x1, Pallas kernels, split_device(): call(functools.partial(project_kernel, n_row, n_col), pltpu.HBM((group, d...  4.77 us
    ppermute x1, waiting for transfers between devices, split_device(): from_xy = lax.ppermute(cond, ('row', 'col'), diag)  2.37 us
    ppermute x1, starting transfers between devices, split_device(): lax.ppermute(to_xy, ('row', 'col'), diag)  1.67 us
    pallas_call x1, Pallas kernels, split_device(): call(functools.partial(score, 1, True), scores, [VMEM] * 4, [held], size=...  1.31 us
  transfers between devices with their start and end apart: 12, of which 11 were waited for; matrix products, arithmetic and copies ran while one was open for 0% of the time, Pallas kernels for 1%

profile of v3, /device:TPU:0, one launch (start us, length us, event | category | flops | bytes accessed | tf_op | source)
XLA Modules:
  0.0 59.4 jit_solution(11189093901939773231)
XLA Ops:
  0.0 4.8 %shard_map.73 = bf16[8,192,128]{2,1,0:T(8,128)(2,1)} custom-call(s32[32]{0:T(128)} %lengths.1, bf16[32,32,2048]{2,1,0:T(8,128)(2,1)} %hidden.1, bf16[64,2048]{1,0:T(8,128)(2,1)} %bitcast.11, bf16[52,32,128]{2,1,0:T(8,128)(2,1)} %grads.1, bf16[52,64]{1,0:T(8,128)(2,1)} %proj_out.1), custom_call_target="tpu_custom_call" | custom-call | flops 268435456 | bytes 4194304 | tf_op jit(solution)/shard_map/pallas_call | solution.py:211
  4.8 13.3 %all_to_all.10.got = bf16[8,192,128]{2,1,0:T(8,128)(2,1)S(1)} all-to-all(bf16[8,192,128]{2,1,0:T(8,128)(2,1)} %shard_map.73), channel_id=1, replica_groups=mesh['row'=4,'col'=2,'store'=4] {'row','col'}, dimensions={0} | all-to-all | bytes 786432 | tf_op jit(solution)/shard_map/all_to_all | solution.py:232
  18.0 1.3 %shard_map.74 = (bf16[32,16,128]{2,1,0:T(8,128)(2,1)}, bf16[512,1024]{1,0:T(8,128)(2,1)S(1)}) custom-call(bf16[8,192,128]{2,1,0:T(8,128)(2,1)S(1)} %all_to_all.10.got, bf16[512,1024]{1,0:T(8,128)(2,1)} %precond.1), custom_call_target="tpu_custom_call" | custom-call | bytes 393216 | tf_op jit(solution)/shard_map/pallas_call | solution.py:236
  19.4 12.3 %all_to_all.11.got = bf16[32,16,128]{2,1,0:T(8,128)(2,1)S(1)} all-to-all(bf16[32,16,128]{2,1,0:T(8,128)(2,1)} %get-tuple-element.13), channel_id=1, replica_groups=mesh['row'=4,'col'=2,'store'=4] {'row','col','store'}, dimensions={0} | all-to-all | bytes 262144 | tf_op jit(solution)/shard_map/all_to_all | solution.py:248
  32.4 1.4 %collective-permute-done.got = f32[2,2,32,512]{3,2,1,0:T(8,128)S(1)} collective-permute-done((f32[2,2,32,512]{3,2,1,0:T(8,128)S(1)}, f32[2,2,32,512]{3,2,1,0:T(8,128)S(1)}, u32[]{:S(2)}, u32[]{:S(2)}) %collective-permute-start) | collective-permute-done | bytes 262176 | tf_op jit(solution)/shard_map/ppermute | solution.py:195
  33.9 0.9 %collective-permute-start.1 = (f32[32,512]{1,0:T(8,128)S(1)}, f32[32,512]{1,0:T(8,128)S(1)}, u32[]{:S(2)}, u32[]{:S(2)}) collective-permute-start(f32[32,512]{1,0:T(8,128)S(1)} %get-tuple-element.18), channel_id=1, source_target_pairs={{0,16},{8,24},{16,0},{24,8},{1,17},{9,25},{17,1},{25,9},{2,18},{10... | collective-permute-start | bytes 196616 | tf_op jit(solution)/shard_map/ppermute | solution.py:195
  34.8 0.9 %collective-permute-start.2 = (f32[32,512]{1,0:T(8,128)S(1)}, f32[32,512]{1,0:T(8,128)S(1)}, u32[]{:S(2)}, u32[]{:S(2)}) collective-permute-start(f32[32,512]{1,0:T(8,128)S(1)} %get-tuple-element.19), channel_id=1, source_target_pairs={{0,4},{4,0},{1,5},{5,1},{2,6},{6,2},{3,7},{7,3},{8,12},{12,8},{9,1... | collective-permute-start | bytes 196616 | tf_op jit(solution)/shard_map/ppermute | solution.py:195
  35.8 1.7 %collective-permute-start.3 = (f32[32,512]{1,0:T(8,128)S(1)}, f32[32,512]{1,0:T(8,128)S(1)}, u32[]{:S(2)}, u32[]{:S(2)}) collective-permute-start(f32[32,512]{1,0:T(8,128)S(1)} %get-tuple-element.20), channel_id=1, source_target_pairs={{0,20},{4,16},{8,28},{12,24},{16,4},{20,0},{24,12},{28,8},{1,21},{... | collective-permute-start | bytes 196616 | tf_op jit(solution)/shard_map/ppermute | solution.py:263
  37.4 0.8 %collective-permute-done.1.refs_1_ = f32[32,512]{1,0:T(8,128)S(1)} collective-permute-done((f32[32,512]{1,0:T(8,128)S(1)}, f32[32,512]{1,0:T(8,128)S(1)}, u32[]{:S(2)}, u32[]{:S(2)}) %collective-permute-start.1) | collective-permute-done | bytes 65568 | tf_op jit(solution)/shard_map/ppermute | solution.py:195
  38.2 1.6 %collective-permute-done.2.refs_2_ = f32[32,512]{1,0:T(8,128)S(1)} collective-permute-done((f32[32,512]{1,0:T(8,128)S(1)}, f32[32,512]{1,0:T(8,128)S(1)}, u32[]{:S(2)}, u32[]{:S(2)}) %collective-permute-start.2) | collective-permute-done | bytes 65568 | tf_op jit(solution)/shard_map/ppermute | solution.py:195
  39.8 1.1 %collective-permute-done.3.refs_3_ = f32[32,512]{1,0:T(8,128)S(1)} collective-permute-done((f32[32,512]{1,0:T(8,128)S(1)}, f32[32,512]{1,0:T(8,128)S(1)}, u32[]{:S(2)}, u32[]{:S(2)}) %collective-permute-start.3) | collective-permute-done | bytes 65568 | tf_op jit(solution)/shard_map/ppermute | solution.py:263
  41.0 1.2 %collective-permute-start.6 = (bf16[32,512]{1,0:T(8,128)(2,1)S(1)}, bf16[32,512]{1,0:T(8,128)(2,1)S(1)}, u32[]{:S(2)}, u32[]{:S(2)}) collective-permute-start(bf16[32,512]{1,0:T(8,128)(2,1)S(1)} %shard_map.77), channel_id=1, source_target_pairs={{0,3},{1,2},{2,1},{3,0},{4,7},{5,6},{6,5},{7,4},{8,11},{9,10},{10,... | collective-permute-start | bytes 98312 | tf_op jit(solution)/shard_map/ppermute | solution.py:195
  42.2 0.8 %collective-permute-start.5 = (bf16[32,512]{1,0:T(8,128)(2,1)S(1)}, bf16[32,512]{1,0:T(8,128)(2,1)S(1)}, u32[]{:S(2)}, u32[]{:S(2)}) collective-permute-start(bf16[32,512]{1,0:T(8,128)(2,1)S(1)} %shard_map.77), channel_id=1, source_target_pairs={{0,2},{1,3},{2,0},{3,1},{4,6},{5,7},{6,4},{7,5},{8,10},{9,11},{10,... | collective-permute-start | bytes 98312 | tf_op jit(solution)/shard_map/ppermute | solution.py:195
  43.0 2.4 %collective-permute-start.4 = (bf16[32,512]{1,0:T(8,128)(2,1)S(1)}, bf16[32,512]{1,0:T(8,128)(2,1)S(1)}, u32[]{:S(2)}, u32[]{:S(2)}) collective-permute-start(bf16[32,512]{1,0:T(8,128)(2,1)S(1)} %shard_map.77), channel_id=1, source_target_pairs={{0,1},{1,0},{2,3},{3,2},{4,5},{5,4},{6,7},{7,6},{8,9},{9,8},{10,11... | collective-permute-start | bytes 98312 | tf_op jit(solution)/shard_map/ppermute | solution.py:195
  45.4 1.3 %collective-permute-done.6 = bf16[32,512]{1,0:T(8,128)(2,1)S(1)} collective-permute-done((bf16[32,512]{1,0:T(8,128)(2,1)S(1)}, bf16[32,512]{1,0:T(8,128)(2,1)S(1)}, u32[]{:S(2)}, u32[]{:S(2)}) %collective-permute-start.6) | collective-permute-done | bytes 32800 | tf_op jit(solution)/shard_map/ppermute | solution.py:195
  46.7 0.8 %collective-permute-done.5 = bf16[32,512]{1,0:T(8,128)(2,1)S(1)} collective-permute-done((bf16[32,512]{1,0:T(8,128)(2,1)S(1)}, bf16[32,512]{1,0:T(8,128)(2,1)S(1)}, u32[]{:S(2)}, u32[]{:S(2)}) %collective-permute-start.5) | collective-permute-done | bytes 32800 | tf_op jit(solution)/shard_map/ppermute | solution.py:195
  47.7 1.5 %collective-permute-start.10 = (bf16[4,32,512]{2,1,0:T(8,128)(2,1)S(1)}, bf16[4,32,512]{2,1,0:T(8,128)(2,1)S(1)}, u32[]{:S(2)}, u32[]{:S(2)}) collective-permute-start(bf16[4,32,512]{2,1,0:T(8,128)(2,1)S(1)} %get-tuple-element.22), channel_id=1, source_target_pairs={{0,16},{8,24},{16,0},{24,8},{1,17},{9,25},{17,1},{25,9},{2,18},{10... | collective-permute-start | bytes 393224 | tf_op jit(solution)/shard_map/ppermute | solution.py:195
  49.2 1.2 %collective-permute-start.8 = (bf16[4,32,512]{2,1,0:T(8,128)(2,1)S(1)}, bf16[4,32,512]{2,1,0:T(8,128)(2,1)S(1)}, u32[]{:S(2)}, u32[]{:S(2)}) collective-permute-start(bf16[4,32,512]{2,1,0:T(8,128)(2,1)S(1)} %get-tuple-element.22), channel_id=1, source_target_pairs={{0,20},{4,16},{8,28},{12,24},{16,4},{20,0},{24,12},{28,8},{1,21},{... | collective-permute-start | bytes 393224 | tf_op jit(solution)/shard_map/ppermute | solution.py:269
  50.4 0.8 %collective-permute-start.7 = (bf16[4,32,512]{2,1,0:T(8,128)(2,1)S(1)}, bf16[4,32,512]{2,1,0:T(8,128)(2,1)S(1)}, u32[]{:S(2)}, u32[]{:S(2)}) collective-permute-start(bf16[4,32,512]{2,1,0:T(8,128)(2,1)S(1)} %get-tuple-element.22), channel_id=1, source_target_pairs={{0,4},{4,0},{1,5},{5,1},{2,6},{6,2},{3,7},{7,3},{8,12},{12,8},{9,1... | collective-permute-start | bytes 393224 | tf_op jit(solution)/shard_map/ppermute | solution.py:195
  51.2 1.5 %collective-permute-done.10 = bf16[4,32,512]{2,1,0:T(8,128)(2,1)S(1)} collective-permute-done((bf16[4,32,512]{2,1,0:T(8,128)(2,1)S(1)}, bf16[4,32,512]{2,1,0:T(8,128)(2,1)S(1)}, u32[]{:S(2)}, u32[]{:S(2)}) %collective-permute-start.10) | collective-permute-done | bytes 131104 | tf_op jit(solution)/shard_map/ppermute | solution.py:195
  52.8 2.4 %collective-permute-done.8 = bf16[4,32,512]{2,1,0:T(8,128)(2,1)S(1)} collective-permute-done((bf16[4,32,512]{2,1,0:T(8,128)(2,1)S(1)}, bf16[4,32,512]{2,1,0:T(8,128)(2,1)S(1)}, u32[]{:S(2)}, u32[]{:S(2)}) %collective-permute-start.8) | collective-permute-done | bytes 131104 | tf_op jit(solution)/shard_map/ppermute | solution.py:269
  55.2 1.3 %collective-permute-done.7 = bf16[4,32,512]{2,1,0:T(8,128)(2,1)S(1)} collective-permute-done((bf16[4,32,512]{2,1,0:T(8,128)(2,1)S(1)}, bf16[4,32,512]{2,1,0:T(8,128)(2,1)S(1)}, u32[]{:S(2)}, u32[]{:S(2)}) %collective-permute-start.7) | collective-permute-done | bytes 131104 | tf_op jit(solution)/shard_map/ppermute | solution.py:195
  57.2 0.9 %collective-permute-done.9.far = bf16[2,4,32,512]{3,2,1,0:T(8,128)(2,1)S(1)} collective-permute-done((bf16[2,4,32,512]{3,2,1,0:T(8,128)(2,1)S(1)}, bf16[2,4,32,512]{3,2,1,0:T(8,128)(2,1)S(1)}, u32[]{:S(2)}, u32[]{:S(2)}) %collective-permute-start.9) | collective-permute-done | bytes 262176 | tf_op jit(solution)/shard_map/ppermute | solution.py:195
  58.1 1.3 %shard_map.79 = f32[128,384]{1,0:T(8,128)} custom-call(bf16[2,4,32,512]{3,2,1,0:T(8,128)(2,1)S(1)} %pad_maximum_fusion.near, bf16[2,4,32,512]{3,2,1,0:T(8,128)(2,1)S(1)} %collective-permute-done.9.far, bf16[384,4096]{1,0:T(8,128)(2,1)S(1)} %copy-done, f32[128,384]{1,0:T(8,128)S(1)} %shard_map.78.refs_0_), custom_call_target="tpu_custom_call" | custom-call | bytes 1572864 | tf_op jit(solution)/shard_map/pallas_call | solution.py:278
  (14 shorter events, 1.7 us)
Async XLA Ops:
  4.8 51.8 %copy-start = (bf16[384,4096]{1,0:T(8,128)(2,1)S(1)}, bf16[384,4096]{1,0:T(8,128)(2,1)}, u32[]{:S(2)}) copy-start(bf16[384,4096]{1,0:T(8,128)(2,1)} %stored.3) | copy-start | bytes 9437188
  32.3 1.6 %collective-permute-start = (f32[2,2,32,512]{3,2,1,0:T(8,128)S(1)}, f32[2,2,32,512]{3,2,1,0:T(8,128)S(1)}, u32[]{:S(2)}, u32[]{:S(2)}) collective-permute-start(f32[2,2,32,512]{3,2,1,0:T(8,128)S(1)} %get-tuple-element.16), channel_id=1, source_target_pairs={{0,8},{8,0},{16,24},{24,16},{1,9},{9,1},{17,25},{25,17},{2,10},{10... | collective-permute-start | bytes 786440 | tf_op jit(solution)/shard_map/ppermute | solution.py:195
  33.9 4.3 %collective-permute-start.1 = (f32[32,512]{1,0:T(8,128)S(1)}, f32[32,512]{1,0:T(8,128)S(1)}, u32[]{:S(2)}, u32[]{:S(2)}) collective-permute-start(f32[32,512]{1,0:T(8,128)S(1)} %get-tuple-element.18), channel_id=1, source_target_pairs={{0,16},{8,24},{16,0},{24,8},{1,17},{9,25},{17,1},{25,9},{2,18},{10... | collective-permute-start | bytes 196616 | tf_op jit(solution)/shard_map/ppermute | solution.py:195
  34.8 5.0 %collective-permute-start.2 = (f32[32,512]{1,0:T(8,128)S(1)}, f32[32,512]{1,0:T(8,128)S(1)}, u32[]{:S(2)}, u32[]{:S(2)}) collective-permute-start(f32[32,512]{1,0:T(8,128)S(1)} %get-tuple-element.19), channel_id=1, source_target_pairs={{0,4},{4,0},{1,5},{5,1},{2,6},{6,2},{3,7},{7,3},{8,12},{12,8},{9,1... | collective-permute-start | bytes 196616 | tf_op jit(solution)/shard_map/ppermute | solution.py:195
  35.8 5.2 %collective-permute-start.3 = (f32[32,512]{1,0:T(8,128)S(1)}, f32[32,512]{1,0:T(8,128)S(1)}, u32[]{:S(2)}, u32[]{:S(2)}) collective-permute-start(f32[32,512]{1,0:T(8,128)S(1)} %get-tuple-element.20), channel_id=1, source_target_pairs={{0,20},{4,16},{8,28},{12,24},{16,4},{20,0},{24,12},{28,8},{1,21},{... | collective-permute-start | bytes 196616 | tf_op jit(solution)/shard_map/ppermute | solution.py:263
  41.0 5.8 %collective-permute-start.6 = (bf16[32,512]{1,0:T(8,128)(2,1)S(1)}, bf16[32,512]{1,0:T(8,128)(2,1)S(1)}, u32[]{:S(2)}, u32[]{:S(2)}) collective-permute-start(bf16[32,512]{1,0:T(8,128)(2,1)S(1)} %shard_map.77), channel_id=1, source_target_pairs={{0,3},{1,2},{2,1},{3,0},{4,7},{5,6},{6,5},{7,4},{8,11},{9,10},{10,... | collective-permute-start | bytes 98312 | tf_op jit(solution)/shard_map/ppermute | solution.py:195
  42.2 5.3 %collective-permute-start.5 = (bf16[32,512]{1,0:T(8,128)(2,1)S(1)}, bf16[32,512]{1,0:T(8,128)(2,1)S(1)}, u32[]{:S(2)}, u32[]{:S(2)}) collective-permute-start(bf16[32,512]{1,0:T(8,128)(2,1)S(1)} %shard_map.77), channel_id=1, source_target_pairs={{0,2},{1,3},{2,0},{3,1},{4,6},{5,7},{6,4},{7,5},{8,10},{9,11},{10,... | collective-permute-start | bytes 98312 | tf_op jit(solution)/shard_map/ppermute | solution.py:195
  43.0 4.6 %collective-permute-start.4 = (bf16[32,512]{1,0:T(8,128)(2,1)S(1)}, bf16[32,512]{1,0:T(8,128)(2,1)S(1)}, u32[]{:S(2)}, u32[]{:S(2)}) collective-permute-start(bf16[32,512]{1,0:T(8,128)(2,1)S(1)} %shard_map.77), channel_id=1, source_target_pairs={{0,1},{1,0},{2,3},{3,2},{4,5},{5,4},{6,7},{7,6},{8,9},{9,8},{10,11... | collective-permute-start | bytes 98312 | tf_op jit(solution)/shard_map/ppermute | solution.py:195
  47.7 5.0 %collective-permute-start.10 = (bf16[4,32,512]{2,1,0:T(8,128)(2,1)S(1)}, bf16[4,32,512]{2,1,0:T(8,128)(2,1)S(1)}, u32[]{:S(2)}, u32[]{:S(2)}) collective-permute-start(bf16[4,32,512]{2,1,0:T(8,128)(2,1)S(1)} %get-tuple-element.22), channel_id=1, source_target_pairs={{0,16},{8,24},{16,0},{24,8},{1,17},{9,25},{17,1},{25,9},{2,18},{10... | collective-permute-start | bytes 393224 | tf_op jit(solution)/shard_map/ppermute | solution.py:195
  49.2 6.0 %collective-permute-start.8 = (bf16[4,32,512]{2,1,0:T(8,128)(2,1)S(1)}, bf16[4,32,512]{2,1,0:T(8,128)(2,1)S(1)}, u32[]{:S(2)}, u32[]{:S(2)}) collective-permute-start(bf16[4,32,512]{2,1,0:T(8,128)(2,1)S(1)} %get-tuple-element.22), channel_id=1, source_target_pairs={{0,20},{4,16},{8,28},{12,24},{16,4},{20,0},{24,12},{28,8},{1,21},{... | collective-permute-start | bytes 393224 | tf_op jit(solution)/shard_map/ppermute | solution.py:269
  50.4 6.1 %collective-permute-start.7 = (bf16[4,32,512]{2,1,0:T(8,128)(2,1)S(1)}, bf16[4,32,512]{2,1,0:T(8,128)(2,1)S(1)}, u32[]{:S(2)}, u32[]{:S(2)}) collective-permute-start(bf16[4,32,512]{2,1,0:T(8,128)(2,1)S(1)} %get-tuple-element.22), channel_id=1, source_target_pairs={{0,4},{4,0},{1,5},{5,1},{2,6},{6,2},{3,7},{7,3},{8,12},{12,8},{9,1... | collective-permute-start | bytes 393224 | tf_op jit(solution)/shard_map/ppermute | solution.py:195
  52.7 3.9 %collective-permute-start.11 = (bf16[2,4,32,512]{3,2,1,0:T(8,128)(2,1)S(1)}, bf16[2,4,32,512]{3,2,1,0:T(8,128)(2,1)S(1)}, u32[]{:S(2)}, u32[]{:S(2)}) collective-permute-start(bf16[2,4,32,512]{3,2,1,0:T(8,128)(2,1)S(1)} %pad_maximum_fusion.1.near), channel_id=1, source_target_pairs={{0,8},{8,0},{16,24},{24,16},{1,9},{9,1},{17,25},{25,17},{2,10},{10... | collective-permute-start | bytes 786440 | tf_op jit(solution)/shard_map/ppermute | solution.py:195
  56.5 1.6 %collective-permute-start.9 = (bf16[2,4,32,512]{3,2,1,0:T(8,128)(2,1)S(1)}, bf16[2,4,32,512]{3,2,1,0:T(8,128)(2,1)S(1)}, u32[]{:S(2)}, u32[]{:S(2)}) collective-permute-start(bf16[2,4,32,512]{3,2,1,0:T(8,128)(2,1)S(1)} %pad_maximum_fusion.near), channel_id=1, source_target_pairs={{0,8},{8,0},{16,24},{24,16},{1,9},{9,1},{17,25},{25,17},{2,10},{10... | collective-permute-start | bytes 786440 | tf_op jit(solution)/shard_map/ppermute | solution.py:195

commit v4 on v3

--- a/solution.py
+++ b/solution.py
@@ -10,6 +10,7 @@
 F32 = jnp.float32
 BF16 = jnp.bfloat16
 AXES = ("row", "col", "store")
+CHIPS = 4
 NT = (((1,), (1,)), ((), ()))
 NN = (((1,), (0,)), ((), ()))
 VMEM = pl.BlockSpec(memory_space=pltpu.VMEM)
@@ -20,24 +21,32 @@
     return lax.dot_general(a, b, dims, preferred_element_type=F32)
 
 
-def project_kernel(n_row, n_col, lengths, hidden, proj_in_t, grads, proj_out, out, *scratch):
-    lengths_s, hidden_s, proj_s, grads_s, weights_s, grads_f32, weights, blocks, sems, chunk_sems, out_sems = scratch
+def offset(k, row, col):
+    return lax.bitwise_xor(row, 2 * (k % 2)), lax.bitwise_xor(col, k // 2)
+
+
+def project_kernel(n_row, n_col, lengths, hidden, proj_in_t, grads, proj_out, *refs):
+    outs, scratch = refs[:CHIPS], refs[CHIPS:]
+    lengths_s, hidden_s, proj_s, grads_s, weights_s, grads_f32, weights, sems, chunk_sems = scratch
     rows, queries, tokens = grads.shape
     columns = hidden.shape[2]
     t_part = hidden.shape[1]
     width = proj_out.shape[1]
     width_in = proj_in_t.shape[0]
-    group = n_row * n_col
-    q_dest = queries // group
+    q_dest = queries // (n_row * n_col)
     share = q_dest // n_col
-    dests = 2
+    row, col = lax.axis_index("row"), lax.axis_index("col")
     pairs = ((proj_in_t, proj_s), (proj_out, weights_s), (grads, grads_s), (lengths, lengths_s))
     small = [pltpu.make_async_copy(src, dst, sems.at[i]) for i, (src, dst) in enumerate(pairs)]
-    chunks = []
-    for i in range(group // dests):
-        part = pl.ds(i * dests * q_dest, dests * q_dest)
-        chunks.append(pltpu.make_async_copy(hidden.at[part], hidden_s.at[part], chunk_sems.at[i]))
-    col = lax.axis_index("col")
+    chunks, starts = [], []
+    for k in range(CHIPS):
+        r, c = offset(k, row, col)
+        for core in range(2):
+            first = ((r // 2 * 2 + core) * n_col + c) * q_dest
+            i = 2 * k + core
+            starts.append(first)
+            part = hidden_s.at[pl.ds(i * q_dest, q_dest)]
+            chunks.append(pltpu.make_async_copy(hidden.at[pl.ds(first, q_dest)], part, chunk_sems.at[i]))
     for copy in small + chunks:
         copy.start()
     small[0].wait()
@@ -51,57 +60,60 @@
     weights[...] = dot(pick.astype(BF16), weights_s[...], NT).astype(BF16)
     grads_f32[...] = grads_s[...].astype(F32).reshape(rows * queries, tokens)
     lane = lax.broadcasted_iota(jnp.int32, (width, tokens), 1)
-    outs = [pltpu.make_async_copy(blocks.at[g], out.at[g], out_sems.at[g]) for g in range(group)]
-    for dest in range(group):
-        for i in range(share):
-            q = dest * q_dest + col * share + i
-            g = grads_f32[pl.ds(q, rows, stride=queries), :].astype(BF16)
-            u = jnp.where(lane < lengths_s[q], dot(weights[...], g, NN), 0.0)
-            at = width_in + i * width
-            blocks[dest, at : at + width, :] = u.astype(BF16)
-        if dest % dests == dests - 1:
-            i = dest // dests
-            chunks[i].wait()
-            part = hidden_s[i * dests * q_dest : (i + 1) * dests * q_dest]
-            v = dot(part.reshape(dests * q_dest * t_part, columns), proj, NN)
-            for k in range(dests):
-                g = i * dests + k
-                blocks[g, 0:width_in, :] = v[k * tokens : (k + 1) * tokens].T.astype(BF16)
-                outs[g].start()
-    for copy in outs:
-        copy.wait()
-
-
-def feature_kernel(n_row, n_col, q_dest, width, width_in, copies, got, precond, out, near, held, made, sem):
+    for k in range(CHIPS):
+        for core in range(2):
+            for i in range(share):
+                q = starts[2 * k + core] + col * share + i
+                g = grads_f32[pl.ds(q, rows, stride=queries), :].astype(BF16)
+                u = jnp.where(lane < lengths_s[q], dot(weights[...], g, NN), 0.0)
+                at = width_in + i * width
+                outs[k][core, at : at + width, :] = u.astype(BF16)
+        chunks[2 * k].wait()
+        chunks[2 * k + 1].wait()
+        part = hidden_s[2 * k * q_dest : 2 * (k + 1) * q_dest]
+        v = dot(part.reshape(2 * q_dest * t_part, columns), proj, NN)
+        for core in range(2):
+            outs[k][core, 0:width_in, :] = v[core * tokens : (core + 1) * tokens].T.astype(BF16)
+
+
+def feature_kernel(n_row, n_col, q_dest, width, width_in, copies, *refs):
+    got, (precond, out, near, held, made, sem) = refs[: 2 * CHIPS], refs[2 * CHIPS :]
     fetch = pltpu.make_async_copy(precond, near, sem.at[1])
     fetch.start()
-    tokens = got.shape[2]
+    tokens = got[0].shape[2]
     t_part = tokens // q_dest
     share = q_dest // n_col
     half = width // 2
     scale = tokens ** (-0.5)
-    lane_v = lax.broadcasted_iota(jnp.int32, (width_in, tokens), 1)
-    parts = [[got[b * n_col + c, 0:width_in, :].astype(F32) for b in range(n_row)] for c in range(n_col)]
+    row, col = lax.axis_index("row"), lax.axis_index("col")
+    core = lax.rem(row, 2)
+    sides = [[] for _ in range(n_col)]
+    for k in range(CHIPS):
+        r, _ = offset(k, row, col)
+        for side in range(2):
+            sides[k // 2].append((lax.bitwise_xor(r, side), got[side * CHIPS + k]))
+    parts = [[(b, ref[core, 0:width_in, :].astype(F32)) for b, ref in sides[c]] for c in range(n_col)]
+    segment = lax.broadcasted_iota(jnp.int32, (width_in, tokens), 1) // t_part
     lane_f = lax.broadcasted_iota(jnp.int32, (half, n_col * width_in), 1)
-    for q in range(q_dest):
-        v_rows = []
-        for c in range(n_col):
-            v = None
-            for b in range(n_row):
-                shift = ((b - q) * t_part) % tokens
-                part = pltpu.roll(parts[c][b], shift, 1) if shift else parts[c][b]
-                v = part if v is None else jnp.where(lane_v >= b * t_part, part, v)
-            v_rows.append(v)
-        v_all = jnp.concatenate(v_rows, axis=0).astype(BF16)
-        at = width_in + (q % share) * width
-        total = None
-        for b in range(n_row):
-            u = got[b * n_col + q // share, at : at + width, :]
-            term = dot(u, v_all, NT)
-            total = term if total is None else total + term
-        total = total + pltpu.roll(total, width_in, 1)
-        packed = jnp.where(lane_f < width_in, total[:half], total[half:]) * scale
-        held[pl.ds(q, half, stride=q_dest), :] = packed
+    for dy in range(n_col):
+        for i in range(share):
+            q = lax.bitwise_xor(col, dy) * share + i
+            v_rows = []
+            for c in range(n_col):
+                v = jnp.zeros((width_in, tokens), F32)
+                for b, part in parts[c]:
+                    shift = lax.rem(b - q + n_row, n_row) * t_part
+                    v = jnp.where(segment == b, pltpu.roll(part, shift, 1), v)
+                v_rows.append(v)
+            v_all = jnp.concatenate(v_rows, axis=0).astype(BF16)
+            at = width_in + i * width
+            total = None
+            for _, ref in sides[dy]:
+                term = dot(ref[core, at : at + width, :], v_all, NT)
+                total = term if total is None else total + term
+            total = total + pltpu.roll(total, width_in, 1)
+            packed = jnp.where(lane_f < width_in, total[:half], total[half:]) * scale
+            held[pl.ds(q, half, stride=q_dest), :] = packed
     group = n_row * n_col
     n = held.shape[0] // group
     for r in range(group):
@@ -195,6 +207,12 @@
     return lax.ppermute(x, axis, [(i, i ^ k) for i in range(n)])
 
 
+def to_chips(arrays, n_row, n_col):
+    diag = [(r * n_col + c, (r ^ 2) * n_col + (c ^ 1)) for r in range(n_row) for c in range(n_col)]
+    own, x, y, xy = arrays
+    return own, swap(x, "row", n_row, 2), swap(y, "col", n_col, 1), lax.ppermute(xy, ("row", "col"), diag)
+
+
 def split_device(sizes, hidden, out_grads, proj_out, proj_in, lengths, precond, stored):
     n_row, n_col, n_store = sizes
     group = n_row * n_col
@@ -210,7 +228,7 @@
     inputs = (lengths, hidden, proj_in.T, out_grads, proj_out)
     blocks = call(
         functools.partial(project_kernel, n_row, n_col),
-        pltpu.HBM((group, depth, tokens), BF16),
+        (shape((2, depth, tokens), BF16),) * CHIPS,
         [HBM] * 5,
         [
             pltpu.SMEM(lengths.shape, jnp.int32),
@@ -220,31 +238,30 @@
             pltpu.VMEM(proj_out.shape, BF16),
             pltpu.VMEM((rows * queries, tokens), F32),
             pltpu.VMEM((width, rows), BF16),
-            pltpu.VMEM((group, depth, tokens), BF16),
             pltpu.SemaphoreType.DMA((4,)),
-            pltpu.SemaphoreType.DMA((group // 2,)),
-            pltpu.SemaphoreType.DMA((group,)),
+            pltpu.SemaphoreType.DMA((2 * CHIPS,)),
         ],
         flops=2 * hidden.size * width_in,
         size=2 * hidden.size,
-        out_specs=HBM,
+        out_specs=(VMEM,) * CHIPS,
     )(*(pltpu.with_memory_space_constraint(a, pltpu.HBM) for a in inputs))
-    got = lax.all_to_all(blocks, ("row", "col"), 0, 0)
+    near = to_chips(blocks, n_row, n_col)
+    far = [swap(a, "row", n_row, 1) for a in near]
 
     half = width // 2
     n = half * q_dest // group
     feats, precond = call(
         functools.partial(feature_kernel, n_row, n_col, q_dest, width, width_in, n_store),
         (pltpu.HBM((group * n_store, n, tokens), BF16), shape(precond.shape, BF16)),
-        [VMEM, HBM],
+        [VMEM] * (2 * CHIPS) + [HBM],
         [
             pltpu.VMEM((half * q_dest, tokens), F32),
             pltpu.VMEM((group * n_store, n, tokens), BF16),
             pltpu.SemaphoreType.DMA((2,)),
         ],
-        size=2 * got.size,
+        size=2 * precond.size,
         out_specs=(HBM, VMEM),
-    )(got, pltpu.with_memory_space_constraint(precond, pltpu.HBM))
+    )(*near, *far, pltpu.with_memory_space_constraint(precond, pltpu.HBM))
     feats = lax.all_to_all(feats, AXES, 0, 0)
 
     sources = group * n_store
@@ -257,16 +274,13 @@
         size=2 * precond.size,
     )(feats, precond)
     got = swap(send, "row", n_row, 1)
-    diag = [(r * n_col + c, (r ^ 2) * n_col + (c ^ 1)) for r in range(n_row) for c in range(n_col)]
     piece = shape((sources, j_width), F32)
-    mine, to_x, to_y, to_xy = call(fold_kernel, (piece,) * 4, [VMEM] * 2, size=keep.size * 8)(keep, got)
-    terms = (mine, swap(to_x, "row", n_row, 2), swap(to_y, "col", n_col, 1), lax.ppermute(to_xy, ("row", "col"), diag))
-    cond = call(finish_kernel, shape(piece.shape, BF16), [VMEM] * 4, size=mine.size * 8)(*terms)
+    terms = call(fold_kernel, (piece,) * 4, [VMEM] * 2, size=keep.size * 8)(keep, got)
+    terms = to_chips(terms, n_row, n_col)
+    cond = call(finish_kernel, shape(piece.shape, BF16), [VMEM] * 4, size=keep.size * 8)(*terms)
 
     cond = jnp.stack([cond] + [swap(cond, "store", n_store, k) for k in range(1, n_store)])
-    from_x = swap(cond, "row", n_row, 2)
-    from_y = swap(cond, "col", n_col, 1)
-    from_xy = lax.ppermute(cond, ("row", "col"), diag)
+    cond, from_x, from_y, from_xy = to_chips([cond] * CHIPS, n_row, n_col)
     scores = shape((sources * q_dest, stored.shape[0]), F32)
     score = functools.partial(score_kernel, n_row, n_col, n_store, q_dest)
     near = jnp.stack([cond, from_x])

time: 59.6 us -> 58 us (0.973)
  blocking collectives: 25.6 us -> 12.4 us
  waiting for transfers between devices: 13.2 us -> 19.9 us
  starting transfers between devices: 11.9 us -> 16.5 us
    all_to_all x1 -> x0, blocking collectives: 13.3 us -> none  [split_device(): got = lax.all_to_all(blocks, ('row', 'col'), 0, 0)]
    ppermute x10 -> x16, waiting for transfers between devices: 9.66 us -> 15.1 us  [swap(): return lax.ppermute(x, axis, [(i, i ^ k) for i in range(n)])]
    ppermute x10 -> x16, starting transfers between devices: 9.05 us -> 13.6 us  [swap(): return lax.ppermute(x, axis, [(i, i ^ k) for i in range(n)])]
    ppermute x2 -> x3, waiting for transfers between devices: 3.51 us -> 4.86 us  [to_chips(): lax.ppermute(xy, ('row', 'col'), diag)]
    ppermute x2 -> x3, starting transfers between devices: 2.83 us -> 2.86 us  [to_chips(): lax.ppermute(xy, ('row', 'col'), diag)]
  transfers between devices with their start and end apart: 12 -> 19, of which waited for: 11 -> 15; matrix products, arithmetic and copies ran while one was open for 0% -> 0% of each run, Pallas kernels for 1% -> 1%
where the time goes in v4:
time: 58 us; the launch traced here: 57.8 us
  waiting for transfers between devices  19.9 us (34%)
  starting transfers between devices  16.5 us (28%)
  blocking collectives  12.4 us (21%)
  Pallas kernels  8.83 us (15%)
    ppermute x16, waiting for transfers between devices, swap(): return lax.ppermute(x, axis, [(i, i ^ k) for i in range(n)])  15.1 us
    ppermute x16, starting transfers between devices, swap(): return lax.ppermute(x, axis, [(i, i ^ k) for i in range(n)])  13.6 us
    all_to_all x1, blocking collectives, split_device(): feats = lax.all_to_all(feats, AXES, 0, 0)  12.4 us
    ppermute x3, waiting for transfers between devices, to_chips(): lax.ppermute(xy, ('row', 'col'), diag)  4.86 us
    pallas_call x1, Pallas kernels, split_device(): call(functools.partial(project_kernel, n_row, n_col), (shape((2, depth, t...  4.55 us
    ppermute x3, starting transfers between devices, to_chips(): lax.ppermute(xy, ('row', 'col'), diag)  2.86 us
    pallas_call x1, Pallas kernels, split_device(): call(functools.partial(feature_kernel, n_row, n_col, q_dest, width, width...  1.73 us
    pallas_call x1, Pallas kernels, split_device(): call(functools.partial(score, 1, True), scores, [VMEM] * 4, [held], size=...  1.31 us
  transfers between devices with their start and end apart: 19, of which 15 were waited for; matrix products, arithmetic and copies ran while one was open for 0% of the time, Pallas kernels for 1%

profile of v4, /device:TPU:0, one launch (start us, length us, event | category | flops | bytes accessed | tf_op | source)
XLA Modules:
  0.0 57.8 jit_solution(12481008181108543733)
XLA Ops:
  0.0 4.5 %shard_map.73 = (bf16[2,192,128]{2,1,0:T(8,128)(2,1)S(1)}, bf16[2,192,128]{2,1,0:T(8,128)(2,1)S(1)}, bf16[2,192,128]{2,1,0:T(8,128)(2,1)S(1)}, bf16[2,192,128]{2,1,0:T(8,128)(2,1)S(1)}) custom-call(s32[32]{0:T(128)} %lengths.1, bf16[32,32,2048]{2,1,0:T(8,128)(2,1)} %hidden.1, bf16[64,2048]{1,0:T(8,128)(2,1)} %bitcast.11, bf16[52,32,128]{2,1,0:T(8,128)(2,1)} %grads.1, ...), custom_call_target="tpu_custom_call" | custom-call | flops 268435456 | bytes 4194304 | tf_op jit(solution)/shard_map/pallas_call | solution.py:229
  4.6 3.0 %collective-permute-start = (bf16[2,192,128]{2,1,0:T(8,128)(2,1)S(1)}, bf16[2,192,128]{2,1,0:T(8,128)(2,1)S(1)}, u32[]{:S(2)}, u32[]{:S(2)}) collective-permute-start(bf16[2,192,128]{2,1,0:T(8,128)(2,1)S(1)} %get-tuple-element.18), channel_id=1, source_target_pairs={{0,16},{8,24},{16,0},{24,8},{1,17},{9,25},{17,1},{25,9},{2,18},{10... | collective-permute-start | bytes 294920 | tf_op jit(solution)/shard_map/ppermute | solution.py:207
  7.6 1.5 %collective-permute-start.1 = (bf16[2,192,128]{2,1,0:T(8,128)(2,1)S(1)}, bf16[2,192,128]{2,1,0:T(8,128)(2,1)S(1)}, u32[]{:S(2)}, u32[]{:S(2)}) collective-permute-start(bf16[2,192,128]{2,1,0:T(8,128)(2,1)S(1)} %get-tuple-element.19), channel_id=1, source_target_pairs={{0,4},{4,0},{1,5},{5,1},{2,6},{6,2},{3,7},{7,3},{8,12},{12,8},{9,1... | collective-permute-start | bytes 294920 | tf_op jit(solution)/shard_map/ppermute | solution.py:207
  9.1 1.5 %collective-permute-done.refs_1_ = bf16[2,192,128]{2,1,0:T(8,128)(2,1)S(1)} collective-permute-done((bf16[2,192,128]{2,1,0:T(8,128)(2,1)S(1)}, bf16[2,192,128]{2,1,0:T(8,128)(2,1)S(1)}, u32[]{:S(2)}, u32[]{:S(2)}) %collective-permute-start) | collective-permute-done | bytes 98336 | tf_op jit(solution)/shard_map/ppermute | solution.py:207
  10.6 2.6 %collective-permute-done.1.refs_2_ = bf16[2,192,128]{2,1,0:T(8,128)(2,1)S(1)} collective-permute-done((bf16[2,192,128]{2,1,0:T(8,128)(2,1)S(1)}, bf16[2,192,128]{2,1,0:T(8,128)(2,1)S(1)}, u32[]{:S(2)}, u32[]{:S(2)}) %collective-permute-start.1) | collective-permute-done | bytes 98336 | tf_op jit(solution)/shard_map/ppermute | solution.py:207
  13.3 1.4 %collective-permute-done.2.refs_3_ = bf16[2,192,128]{2,1,0:T(8,128)(2,1)S(1)} collective-permute-done((bf16[2,192,128]{2,1,0:T(8,128)(2,1)S(1)}, bf16[2,192,128]{2,1,0:T(8,128)(2,1)S(1)}, u32[]{:S(2)}, u32[]{:S(2)}) %collective-permute-start.2) | collective-permute-done | bytes 98336 | tf_op jit(solution)/shard_map/ppermute | solution.py:213
  14.6 1.3 %collective-permute-done.6.refs_7_ = bf16[2,192,128]{2,1,0:T(8,128)(2,1)S(1)} collective-permute-done((bf16[2,192,128]{2,1,0:T(8,128)(2,1)S(1)}, bf16[2,192,128]{2,1,0:T(8,128)(2,1)S(1)}, u32[]{:S(2)}, u32[]{:S(2)}) %collective-permute-start.6) | collective-permute-done | bytes 98336 | tf_op jit(solution)/shard_map/ppermute | solution.py:207
  15.9 1.7 %shard_map.74 = (bf16[32,16,128]{2,1,0:T(8,128)(2,1)}, bf16[512,1024]{1,0:T(8,128)(2,1)S(1)}) custom-call(bf16[2,192,128]{2,1,0:T(8,128)(2,1)S(1)} %get-tuple-element.17.refs_0_, bf16[2,192,128]{2,1,0:T(8,128)(2,1)S(1)} %collective-permute-done.refs_1_, bf16[2,192,128]{2,1,0:T(8,128)(2,1)S(1)} %collective-permute-done.1.refs_2_, ...), custom_call_target="tpu_custom_call" | custom-call | bytes 1048576 | tf_op jit(solution)/shard_map/pallas_call | solution.py:253
  17.6 12.4 %all_to_all.5.got = bf16[32,16,128]{2,1,0:T(8,128)(2,1)S(1)} all-to-all(bf16[32,16,128]{2,1,0:T(8,128)(2,1)} %get-tuple-element.21), channel_id=1, replica_groups=mesh['row'=4,'col'=2,'store'=4] {'row','col','store'}, dimensions={0} | all-to-all | bytes 262144 | tf_op jit(solution)/shard_map/all_to_all | solution.py:265
  30.8 1.4 %collective-permute-done.7.got = f32[2,2,32,512]{3,2,1,0:T(8,128)S(1)} collective-permute-done((f32[2,2,32,512]{3,2,1,0:T(8,128)S(1)}, f32[2,2,32,512]{3,2,1,0:T(8,128)S(1)}, u32[]{:S(2)}, u32[]{:S(2)}) %collective-permute-start.7) | collective-permute-done | bytes 262176 | tf_op jit(solution)/shard_map/ppermute | solution.py:207
  32.3 0.9 %collective-permute-start.8 = (f32[32,512]{1,0:T(8,128)S(1)}, f32[32,512]{1,0:T(8,128)S(1)}, u32[]{:S(2)}, u32[]{:S(2)}) collective-permute-start(f32[32,512]{1,0:T(8,128)S(1)} %get-tuple-element.26), channel_id=1, source_target_pairs={{0,16},{8,24},{16,0},{24,8},{1,17},{9,25},{17,1},{25,9},{2,18},{10... | collective-permute-start | bytes 196616 | tf_op jit(solution)/shard_map/ppermute | solution.py:207
  33.2 0.9 %collective-permute-start.9 = (f32[32,512]{1,0:T(8,128)S(1)}, f32[32,512]{1,0:T(8,128)S(1)}, u32[]{:S(2)}, u32[]{:S(2)}) collective-permute-start(f32[32,512]{1,0:T(8,128)S(1)} %get-tuple-element.27), channel_id=1, source_target_pairs={{0,4},{4,0},{1,5},{5,1},{2,6},{6,2},{3,7},{7,3},{8,12},{12,8},{9,1... | collective-permute-start | bytes 196616 | tf_op jit(solution)/shard_map/ppermute | solution.py:207
  34.2 1.7 %collective-permute-start.10 = (f32[32,512]{1,0:T(8,128)S(1)}, f32[32,512]{1,0:T(8,128)S(1)}, u32[]{:S(2)}, u32[]{:S(2)}) collective-permute-start(f32[32,512]{1,0:T(8,128)S(1)} %get-tuple-element.28), channel_id=1, source_target_pairs={{0,20},{4,16},{8,28},{12,24},{16,4},{20,0},{24,12},{28,8},{1,21},{... | collective-permute-start | bytes 196616 | tf_op jit(solution)/shard_map/ppermute | solution.py:213
  36.6 1.6 %collective-permute-done.9.refs_2_ = f32[32,512]{1,0:T(8,128)S(1)} collective-permute-done((f32[32,512]{1,0:T(8,128)S(1)}, f32[32,512]{1,0:T(8,128)S(1)}, u32[]{:S(2)}, u32[]{:S(2)}) %collective-permute-start.9) | collective-permute-done | bytes 65568 | tf_op jit(solution)/shard_map/ppermute | solution.py:207
  38.2 1.1 %collective-permute-done.10.refs_3_ = f32[32,512]{1,0:T(8,128)S(1)} collective-permute-done((f32[32,512]{1,0:T(8,128)S(1)}, f32[32,512]{1,0:T(8,128)S(1)}, u32[]{:S(2)}, u32[]{:S(2)}) %collective-permute-start.10) | collective-permute-done | bytes 65568 | tf_op jit(solution)/shard_map/ppermute | solution.py:213
  39.4 1.2 %collective-permute-start.13 = (bf16[32,512]{1,0:T(8,128)(2,1)S(1)}, bf16[32,512]{1,0:T(8,128)(2,1)S(1)}, u32[]{:S(2)}, u32[]{:S(2)}) collective-permute-start(bf16[32,512]{1,0:T(8,128)(2,1)S(1)} %shard_map.77), channel_id=1, source_target_pairs={{0,3},{1,2},{2,1},{3,0},{4,7},{5,6},{6,5},{7,4},{8,11},{9,10},{10,... | collective-permute-start | bytes 98312 | tf_op jit(solution)/shard_map/ppermute | solution.py:207
  41.4 2.4 %collective-permute-start.11 = (bf16[32,512]{1,0:T(8,128)(2,1)S(1)}, bf16[32,512]{1,0:T(8,128)(2,1)S(1)}, u32[]{:S(2)}, u32[]{:S(2)}) collective-permute-start(bf16[32,512]{1,0:T(8,128)(2,1)S(1)} %shard_map.77), channel_id=1, source_target_pairs={{0,1},{1,0},{2,3},{3,2},{4,5},{5,4},{6,7},{7,6},{8,9},{9,8},{10,11... | collective-permute-start | bytes 98312 | tf_op jit(solution)/shard_map/ppermute | solution.py:207
  43.8 1.3 %collective-permute-done.13 = bf16[32,512]{1,0:T(8,128)(2,1)S(1)} collective-permute-done((bf16[32,512]{1,0:T(8,128)(2,1)S(1)}, bf16[32,512]{1,0:T(8,128)(2,1)S(1)}, u32[]{:S(2)}, u32[]{:S(2)}) %collective-permute-start.13) | collective-permute-done | bytes 32800 | tf_op jit(solution)/shard_map/ppermute | solution.py:207
  46.1 1.5 %collective-permute-start.17 = (bf16[4,32,512]{2,1,0:T(8,128)(2,1)S(1)}, bf16[4,32,512]{2,1,0:T(8,128)(2,1)S(1)}, u32[]{:S(2)}, u32[]{:S(2)}) collective-permute-start(bf16[4,32,512]{2,1,0:T(8,128)(2,1)S(1)} %get-tuple-element.30), channel_id=1, source_target_pairs={{0,16},{8,24},{16,0},{24,8},{1,17},{9,25},{17,1},{25,9},{2,18},{10... | collective-permute-start | bytes 393224 | tf_op jit(solution)/shard_map/ppermute | solution.py:207
  47.6 1.2 %collective-permute-start.15 = (bf16[4,32,512]{2,1,0:T(8,128)(2,1)S(1)}, bf16[4,32,512]{2,1,0:T(8,128)(2,1)S(1)}, u32[]{:S(2)}, u32[]{:S(2)}) collective-permute-start(bf16[4,32,512]{2,1,0:T(8,128)(2,1)S(1)} %get-tuple-element.30), channel_id=1, source_target_pairs={{0,20},{4,16},{8,28},{12,24},{16,4},{20,0},{24,12},{28,8},{1,21},{... | collective-permute-start | bytes 393224 | tf_op jit(solution)/shard_map/ppermute | solution.py:213
  49.6 1.5 %collective-permute-done.17 = bf16[4,32,512]{2,1,0:T(8,128)(2,1)S(1)} collective-permute-done((bf16[4,32,512]{2,1,0:T(8,128)(2,1)S(1)}, bf16[4,32,512]{2,1,0:T(8,128)(2,1)S(1)}, u32[]{:S(2)}, u32[]{:S(2)}) %collective-permute-start.17) | collective-permute-done | bytes 131104 | tf_op jit(solution)/shard_map/ppermute | solution.py:207
  51.2 2.4 %collective-permute-done.15 = bf16[4,32,512]{2,1,0:T(8,128)(2,1)S(1)} collective-permute-done((bf16[4,32,512]{2,1,0:T(8,128)(2,1)S(1)}, bf16[4,32,512]{2,1,0:T(8,128)(2,1)S(1)}, u32[]{:S(2)}, u32[]{:S(2)}) %collective-permute-start.15) | collective-permute-done | bytes 131104 | tf_op jit(solution)/shard_map/ppermute | solution.py:213
  53.6 1.3 %collective-permute-done.14 = bf16[4,32,512]{2,1,0:T(8,128)(2,1)S(1)} collective-permute-done((bf16[4,32,512]{2,1,0:T(8,128)(2,1)S(1)}, bf16[4,32,512]{2,1,0:T(8,128)(2,1)S(1)}, u32[]{:S(2)}, u32[]{:S(2)}) %collective-permute-start.14) | collective-permute-done | bytes 131104 | tf_op jit(solution)/shard_map/ppermute | solution.py:207
  56.5 1.3 %shard_map.79 = f32[128,384]{1,0:T(8,128)} custom-call(bf16[2,4,32,512]{3,2,1,0:T(8,128)(2,1)S(1)} %pad_maximum_fusion.near, bf16[2,4,32,512]{3,2,1,0:T(8,128)(2,1)S(1)} %collective-permute-done.16.far, bf16[384,4096]{1,0:T(8,128)(2,1)S(1)} %copy-done, f32[128,384]{1,0:T(8,128)S(1)} %shard_map.78.refs_0_), custom_call_target="tpu_custom_call" | custom-call | bytes 1572864 | tf_op jit(solution)/shard_map/pallas_call | solution.py:292
  (27 shorter events, 5.9 us)
Async XLA Ops:
  0.0 55.0 %copy-start = (bf16[384,4096]{1,0:T(8,128)(2,1)S(1)}, bf16[384,4096]{1,0:T(8,128)(2,1)}, u32[]{:S(2)}) copy-start(bf16[384,4096]{1,0:T(8,128)(2,1)} %stored.3) | copy-start | bytes 9437188
  4.6 6.1 %collective-permute-start = (bf16[2,192,128]{2,1,0:T(8,128)(2,1)S(1)}, bf16[2,192,128]{2,1,0:T(8,128)(2,1)S(1)}, u32[]{:S(2)}, u32[]{:S(2)}) collective-permute-start(bf16[2,192,128]{2,1,0:T(8,128)(2,1)S(1)} %get-tuple-element.18), channel_id=1, source_target_pairs={{0,16},{8,24},{16,0},{24,8},{1,17},{9,25},{17,1},{25,9},{2,18},{10... | collective-permute-start | bytes 294920 | tf_op jit(solution)/shard_map/ppermute | solution.py:207
  7.6 5.7 %collective-permute-start.1 = (bf16[2,192,128]{2,1,0:T(8,128)(2,1)S(1)}, bf16[2,192,128]{2,1,0:T(8,128)(2,1)S(1)}, u32[]{:S(2)}, u32[]{:S(2)}) collective-permute-start(bf16[2,192,128]{2,1,0:T(8,128)(2,1)S(1)} %get-tuple-element.19), channel_id=1, source_target_pairs={{0,4},{4,0},{1,5},{5,1},{2,6},{6,2},{3,7},{7,3},{8,12},{12,8},{9,1... | collective-permute-start | bytes 294920 | tf_op jit(solution)/shard_map/ppermute | solution.py:207
  9.1 5.5 %collective-permute-start.2 = (bf16[2,192,128]{2,1,0:T(8,128)(2,1)S(1)}, bf16[2,192,128]{2,1,0:T(8,128)(2,1)S(1)}, u32[]{:S(2)}, u32[]{:S(2)}) collective-permute-start(bf16[2,192,128]{2,1,0:T(8,128)(2,1)S(1)} %get-tuple-element.20), channel_id=1, source_target_pairs={{0,20},{4,16},{8,28},{12,24},{16,4},{20,0},{24,12},{28,8},{1,21},{... | collective-permute-start | bytes 294920 | tf_op jit(solution)/shard_map/ppermute | solution.py:213
  9.1 5.5 %collective-permute-start.3 = (bf16[2,192,128]{2,1,0:T(8,128)(2,1)S(1)}, bf16[2,192,128]{2,1,0:T(8,128)(2,1)S(1)}, u32[]{:S(2)}, u32[]{:S(2)}) collective-permute-start(bf16[2,192,128]{2,1,0:T(8,128)(2,1)S(1)} %get-tuple-element.17.refs_0_), channel_id=1, source_target_pairs={{0,8},{8,0},{16,24},{24,16},{1,9},{9,1},{17,25},{25,17},{2,10},{10... | collective-permute-start | bytes 294920 | tf_op jit(solution)/shard_map/ppermute | solution.py:207
  10.6 4.0 %collective-permute-start.4 = (bf16[2,192,128]{2,1,0:T(8,128)(2,1)S(1)}, bf16[2,192,128]{2,1,0:T(8,128)(2,1)S(1)}, u32[]{:S(2)}, u32[]{:S(2)}) collective-permute-start(bf16[2,192,128]{2,1,0:T(8,128)(2,1)S(1)} %collective-permute-done.refs_1_), channel_id=1, source_target_pairs={{0,8},{8,0},{16,24},{24,16},{1,9},{9,1},{17,25},{25,17},{2,10},{10... | collective-permute-start | bytes 294920 | tf_op jit(solution)/shard_map/ppermute | solution.py:207
  13.3 1.4 %collective-permute-start.5 = (bf16[2,192,128]{2,1,0:T(8,128)(2,1)S(1)}, bf16[2,192,128]{2,1,0:T(8,128)(2,1)S(1)}, u32[]{:S(2)}, u32[]{:S(2)}) collective-permute-start(bf16[2,192,128]{2,1,0:T(8,128)(2,1)S(1)} %collective-permute-done.1.refs_2_), channel_id=1, source_target_pairs={{0,8},{8,0},{16,24},{24,16},{1,9},{9,1},{17,25},{25,17},{2,10},{10... | collective-permute-start | bytes 294920 | tf_op jit(solution)/shard_map/ppermute | solution.py:207
  14.6 1.3 %collective-permute-start.6 = (bf16[2,192,128]{2,1,0:T(8,128)(2,1)S(1)}, bf16[2,192,128]{2,1,0:T(8,128)(2,1)S(1)}, u32[]{:S(2)}, u32[]{:S(2)}) collective-permute-start(bf16[2,192,128]{2,1,0:T(8,128)(2,1)S(1)} %collective-permute-done.2.refs_3_), channel_id=1, source_target_pairs={{0,8},{8,0},{16,24},{24,16},{1,9},{9,1},{17,25},{25,17},{2,10},{10... | collective-permute-start | bytes 294920 | tf_op jit(solution)/shard_map/ppermute | solution.py:207
  30.7 1.6 %collective-permute-start.7 = (f32[2,2,32,512]{3,2,1,0:T(8,128)S(1)}, f32[2,2,32,512]{3,2,1,0:T(8,128)S(1)}, u32[]{:S(2)}, u32[]{:S(2)}) collective-permute-start(f32[2,2,32,512]{3,2,1,0:T(8,128)S(1)} %get-tuple-element.24), channel_id=1, source_target_pairs={{0,8},{8,0},{16,24},{24,16},{1,9},{9,1},{17,25},{25,17},{2,10},{10... | collective-permute-start | bytes 786440 | tf_op jit(solution)/shard_map/ppermute | solution.py:207
  32.3 4.3 %collective-permute-start.8 = (f32[32,512]{1,0:T(8,128)S(1)}, f32[32,512]{1,0:T(8,128)S(1)}, u32[]{:S(2)}, u32[]{:S(2)}) collective-permute-start(f32[32,512]{1,0:T(8,128)S(1)} %get-tuple-element.26), channel_id=1, source_target_pairs={{0,16},{8,24},{16,0},{24,8},{1,17},{9,25},{17,1},{25,9},{2,18},{10... | collective-permute-start | bytes 196616 | tf_op jit(solution)/shard_map/ppermute | solution.py:207
  33.2 5.0 %collective-permute-start.9 = (f32[32,512]{1,0:T(8,128)S(1)}, f32[32,512]{1,0:T(8,128)S(1)}, u32[]{:S(2)}, u32[]{:S(2)}) collective-permute-start(f32[32,512]{1,0:T(8,128)S(1)} %get-tuple-element.27), channel_id=1, source_target_pairs={{0,4},{4,0},{1,5},{5,1},{2,6},{6,2},{3,7},{7,3},{8,12},{12,8},{9,1... | collective-permute-start | bytes 196616 | tf_op jit(solution)/shard_map/ppermute | solution.py:207
  34.2 5.2 %collective-permute-start.10 = (f32[32,512]{1,0:T(8,128)S(1)}, f32[32,512]{1,0:T(8,128)S(1)}, u32[]{:S(2)}, u32[]{:S(2)}) collective-permute-start(f32[32,512]{1,0:T(8,128)S(1)} %get-tuple-element.28), channel_id=1, source_target_pairs={{0,20},{4,16},{8,28},{12,24},{16,4},{20,0},{24,12},{28,8},{1,21},{... | collective-permute-start | bytes 196616 | tf_op jit(solution)/shard_map/ppermute | solution.py:213
  39.4 5.8 %collective-permute-start.13 = (bf16[32,512]{1,0:T(8,128)(2,1)S(1)}, bf16[32,512]{1,0:T(8,128)(2,1)S(1)}, u32[]{:S(2)}, u32[]{:S(2)}) collective-permute-start(bf16[32,512]{1,0:T(8,128)(2,1)S(1)} %shard_map.77), channel_id=1, source_target_pairs={{0,3},{1,2},{2,1},{3,0},{4,7},{5,6},{6,5},{7,4},{8,11},{9,10},{10,... | collective-permute-start | bytes 98312 | tf_op jit(solution)/shard_map/ppermute | solution.py:207
  40.6 5.3 %collective-permute-start.12 = (bf16[32,512]{1,0:T(8,128)(2,1)S(1)}, bf16[32,512]{1,0:T(8,128)(2,1)S(1)}, u32[]{:S(2)}, u32[]{:S(2)}) collective-permute-start(bf16[32,512]{1,0:T(8,128)(2,1)S(1)} %shard_map.77), channel_id=1, source_target_pairs={{0,2},{1,3},{2,0},{3,1},{4,6},{5,7},{6,4},{7,5},{8,10},{9,11},{10,... | collective-permute-start | bytes 98312 | tf_op jit(solution)/shard_map/ppermute | solution.py:207
  41.4 4.6 %collective-permute-start.11 = (bf16[32,512]{1,0:T(8,128)(2,1)S(1)}, bf16[32,512]{1,0:T(8,128)(2,1)S(1)}, u32[]{:S(2)}, u32[]{:S(2)}) collective-permute-start(bf16[32,512]{1,0:T(8,128)(2,1)S(1)} %shard_map.77), channel_id=1, source_target_pairs={{0,1},{1,0},{2,3},{3,2},{4,5},{5,4},{6,7},{7,6},{8,9},{9,8},{10,11... | collective-permute-start | bytes 98312 | tf_op jit(solution)/shard_map/ppermute | solution.py:207
  46.1 5.0 %collective-permute-start.17 = (bf16[4,32,512]{2,1,0:T(8,128)(2,1)S(1)}, bf16[4,32,512]{2,1,0:T(8,128)(2,1)S(1)}, u32[]{:S(2)}, u32[]{:S(2)}) collective-permute-start(bf16[4,32,512]{2,1,0:T(8,128)(2,1)S(1)} %get-tuple-element.30), channel_id=1, source_target_pairs={{0,16},{8,24},{16,0},{24,8},{1,17},{9,25},{17,1},{25,9},{2,18},{10... | collective-permute-start | bytes 393224 | tf_op jit(solution)/shard_map/ppermute | solution.py:207
  47.6 6.0 %collective-permute-start.15 = (bf16[4,32,512]{2,1,0:T(8,128)(2,1)S(1)}, bf16[4,32,512]{2,1,0:T(8,128)(2,1)S(1)}, u32[]{:S(2)}, u32[]{:S(2)}) collective-permute-start(bf16[4,32,512]{2,1,0:T(8,128)(2,1)S(1)} %get-tuple-element.30), channel_id=1, source_target_pairs={{0,20},{4,16},{8,28},{12,24},{16,4},{20,0},{24,12},{28,8},{1,21},{... | collective-permute-start | bytes 393224 | tf_op jit(solution)/shard_map/ppermute | solution.py:213
  48.8 6.1 %collective-permute-start.14 = (bf16[4,32,512]{2,1,0:T(8,128)(2,1)S(1)}, bf16[4,32,512]{2,1,0:T(8,128)(2,1)S(1)}, u32[]{:S(2)}, u32[]{:S(2)}) collective-permute-start(bf16[4,32,512]{2,1,0:T(8,128)(2,1)S(1)} %get-tuple-element.30), channel_id=1, source_target_pairs={{0,4},{4,0},{1,5},{5,1},{2,6},{6,2},{3,7},{7,3},{8,12},{12,8},{9,1... | collective-permute-start | bytes 393224 | tf_op jit(solution)/shard_map/ppermute | solution.py:207
  51.1 3.9 %collective-permute-start.18 = (bf16[2,4,32,512]{3,2,1,0:T(8,128)(2,1)S(1)}, bf16[2,4,32,512]{3,2,1,0:T(8,128)(2,1)S(1)}, u32[]{:S(2)}, u32[]{:S(2)}) collective-permute-start(bf16[2,4,32,512]{3,2,1,0:T(8,128)(2,1)S(1)} %pad_maximum_fusion.1.near), channel_id=1, source_target_pairs={{0,8},{8,0},{16,24},{24,16},{1,9},{9,1},{17,25},{25,17},{2,10},{10... | collective-permute-start | bytes 786440 | tf_op jit(solution)/shard_map/ppermute | solution.py:207
  54.9 1.6 %collective-permute-start.16 = (bf16[2,4,32,512]{3,2,1,0:T(8,128)(2,1)S(1)}, bf16[2,4,32,512]{3,2,1,0:T(8,128)(2,1)S(1)}, u32[]{:S(2)}, u32[]{:S(2)}) collective-permute-start(bf16[2,4,32,512]{3,2,1,0:T(8,128)(2,1)S(1)} %pad_maximum_fusion.near), channel_id=1, source_target_pairs={{0,8},{8,0},{16,24},{24,16},{1,9},{9,1},{17,25},{25,17},{2,10},{10... | collective-permute-start | bytes 786440 | tf_op jit(solution)/shard_map/ppermute | solution.py:207
